TPU v7x, 256 devices: a whole 4x4x8 slice. The times are simulated.
256 devices in a mesh: grid: 4 (over x), span: 4 (over y), normal: 16 (over z, core).
Axes of the slice: x: 4, y: 4, z: 8, core: 2. Of those that a mesh axis runs over, the one named last changes fastest.
Arguments:
- state: float32 [5, 4, 256, 4096], P(None, 'grid', 'normal', 'span'), may hold values from -6 to 6
- iblank: int32 [4, 256, 4096], P('grid', 'normal', 'span'), may hold values 0 or 1
- flux: float32 [5, 5, 4], P(None, None, 'grid'), may hold values from -3 to 3
- left_vectors: float32 [5, 5, 4, 4096], P(None, None, 'grid', 'span')
- right_vectors: float32 [5, 5, 4, 4096], P(None, None, 'grid', 'span')
- low_one: float32 [5, 4, 256, 4096], P(None, 'grid', 'normal', 'span'), as said below
- low_two: float32 [5, 4, 256, 4096], P(None, 'grid', 'normal', 'span')
- up_one: float32 [5, 4, 256, 4096], P(None, 'grid', 'normal', 'span')
- up_two: float32 [5, 4, 256, 4096], P(None, 'grid', 'normal', 'span')
- pivot: float32 [5, 4, 256, 4096], P(None, 'grid', 'normal', 'span')
- donor_cells: int32 [8, 4, 384, 512], P(None, 'grid', 'normal', 'span'), may hold values from 0 to 16383
- donor_weights: float32 [8, 4, 384, 512], P(None, 'grid', 'normal', 'span'), as said below
- fringe_cells: int32 [4, 384, 512], P('grid', 'normal', 'span'), may hold values from 0 to 16383, as said below
- fringe_live: int32 [4, 384, 512], P('grid', 'normal', 'span'), may hold values from 0 to 1, as said below
Outputs:
- updated: float32 [5, 4, 256, 4096], P(None, 'grid', 'normal', 'span')
Inputs may be any that keep to these rules, and one draw needn't show every extreme that they name: In every cell |low_one| + |low_two| < 1 and |up_one| + |up_two| < 1, with low_one and up_one negative. `donor_weights`: each slot's eight weights are the trilinear weights of a point in a unit cell: nonnegative, summing to one. `fringe_cells`: on one device, the 3072 slots name distinct local cells. `fringe_live`: within the slots of one source grid on one device, the first k blocks are live and the others not, k from 1 to 6, and 0 for a grid's own slots; on every device some source grid has all 6 blocks live.
All inputs are finite; a program needn't handle non-finite values. No bound on the sum of `iblank` on one device may be relied on, other than what follows from the above.
Results may differ from a plain program's by a relative error of at most 0.0003.
Values sent between devices are 32-bit elements; how exact they have to be, the bound alone decides.
A program may use at most 128 MiB of HBM per device.

v0:
```python
import jax
import jax.numpy as jnp
from jax import lax
from jax.sharding import Mesh
from jax.sharding import PartitionSpec as P

ITERS = 2
NORMAL = ("normal_0", "normal_1")


DISSIP = 0.06
STEP = 0.4


def carried_in(part, axis, combine, identity):
    place = lax.axis_index(axis)
    gathered = jax.tree.map(lambda a: lax.all_gather(a, axis), part)
    state = jax.tree.map(lambda a, e: jnp.zeros_like(a) + jnp.asarray(e, a.dtype), part, identity)

    def one(step, state):
        return combine(
            state, jax.tree.map(lambda a: lax.dynamic_index_in_dim(a, step, 0, False), gathered)
        )

    return lax.fori_loop(0, place, one, state)


def filled_with(value, identity):
    return jax.tree.map(
        lambda part, zero: jnp.zeros_like(part) + jnp.asarray(zero, part.dtype), value, identity
    )


def gathered_once(value, axis):
    leaves = jax.tree.leaves(value)
    sequence = sorted(range(len(leaves)), key=lambda k: -leaves[k].size)
    width = (1, *leaves[sequence[0]].shape)[-1]
    lines = [
        jnp.pad(leaves[k].reshape(-1), (0, -leaves[k].size % width)).reshape(-1, width)
        for k in sequence
    ]
    both, at, found = (lax.all_gather(jnp.concatenate(lines), axis), 0, {})
    for k, line in zip(sequence, lines):
        share = both[:, at : at + len(line)].reshape(len(both), -1)
        found[k] = share[:, : leaves[k].size].reshape(-1, *leaves[k].shape)
        at += len(line)
    numbers = iter(range(len(leaves)))
    return jax.tree.map(lambda _: found[next(numbers)], value)


def once_a_type(value, axis):
    leaves, found = (jax.tree.leaves(value), {})
    for first, a in enumerate(leaves):
        if first not in found:
            alike = [k for k, b in enumerate(leaves) if b.dtype == a.dtype]
            got = (
                gathered_once([leaves[k] for k in alike], axis)
                if len(alike) > 1
                else [lax.all_gather(a, axis)]
            )
            for k, b in zip(alike, got):
                found[k] = b
    numbers = iter(range(len(leaves)))
    return jax.tree.map(lambda _: found[next(numbers)], value)


def prefix_by_axis(value, axes, combine, identity):
    before = start = filled_with(value, identity)
    subtotal = value
    for axis in reversed(axes):
        length, place = (lax.axis_size(axis), lax.axis_index(axis))
        pieces = once_a_type(subtotal, axis)
        inside, subtotal = (start, start)
        for k in reversed(range(length)):
            passed = k > place
            subtotal = combine(subtotal, jax.tree.map(lambda part: part[k], pieces))
            inside = jax.tree.map(lambda new, old: jnp.where(passed, new, old), subtotal, inside)
        before = combine(inside, before)
    return before


def extended(value, sides, width):
    for axis, dim in sides:
        size, length = (lax.axis_size(axis), value.shape[dim])
        up = [(i, (i + 1) % size) for i in range(size - 1)]
        down = [(j, i) for i, j in up]
        last = lax.slice_in_dim(value, length - width, length, axis=dim)
        first = lax.slice_in_dim(value, 0, width, axis=dim)
        before = lax.ppermute(last, axis, up)
        after = lax.ppermute(first, axis, down)
        value = jnp.concatenate([before, value, after], axis=dim)
    return value


def compose(earlier, later):
    return (
        later[0] * earlier[0] + later[1] * earlier[2],
        later[0] * earlier[1] + later[1] * earlier[3],
        later[2] * earlier[0] + later[3] * earlier[2],
        later[2] * earlier[1] + later[3] * earlier[3],
        later[0] * earlier[4] + later[1] * earlier[5] + later[4],
        later[2] * earlier[4] + later[3] * earlier[5] + later[5],
    )


def identity_map(sample):
    unit_ones = jnp.ones_like(sample)
    empty_part = jnp.zeros_like(sample)
    return (unit_ones, empty_part, empty_part, unit_ones, empty_part, empty_part)


def small_matrix(matrix, values):
    rows = []
    for out_index in range(5):
        total = matrix[out_index, 0] * values[0]
        for inner in range(1, 5):
            total = total + matrix[out_index, inner] * values[inner]
        rows.append(total)
    return jnp.stack(rows)


def residual_of(padded, mixing):
    center = padded[..., 2:-2, 2:-2]
    central = padded[..., 2:-2, 3:-1] - padded[..., 2:-2, 1:-3]
    normal_fourth = (
        padded[..., 4:, 2:-2]
        - 4.0 * padded[..., 3:-1, 2:-2]
        + 6.0 * center
        - 4.0 * padded[..., 1:-3, 2:-2]
        + padded[..., :-4, 2:-2]
    )
    span_fourth = (
        padded[..., 2:-2, 4:]
        - 4.0 * padded[..., 2:-2, 3:-1]
        + 6.0 * center
        - 4.0 * padded[..., 2:-2, 1:-3]
        + padded[..., 2:-2, :-4]
    )
    transported = small_matrix(mixing, central)
    return -0.5 * transported - DISSIP * (normal_fourth + span_fourth)


def linear_pass(first, second, source, reverse, connect):
    row_sample = source[:, 0]
    unit_ones = jnp.ones_like(row_sample)
    empty_part = jnp.zeros_like(row_sample)

    def advance(carried, inputs):
        base_now, base_prev, one_now, one_prev, two_now, two_prev = carried
        value, coef_one, coef_two = inputs
        base_next = value - coef_one * base_now - coef_two * base_prev
        one_next = -coef_one * one_now - coef_two * one_prev
        two_next = -coef_one * two_now - coef_two * two_prev
        return (
            (base_next, base_now, one_next, one_now, two_next, two_now),
            (base_next, one_next, two_next),
        )

    start = (empty_part, empty_part, unit_ones, empty_part, empty_part, unit_ones)
    moved = tuple((jnp.moveaxis(member, 1, 0) for member in (source, first, second)))
    final, outputs = lax.scan(advance, start, moved, reverse=reverse)
    base_rows, one_rows, two_rows = outputs
    totals = (final[2], final[4], final[3], final[5], final[0], final[1])
    entering = connect(totals)
    result = one_rows * entering[0][None] + two_rows * entering[1][None] + base_rows
    return jnp.moveaxis(result, 0, 1)


def forward_link(totals):
    incoming = carried_in(totals, NORMAL, compose, identity_map(totals[0]))
    return (incoming[4], incoming[5])


def backward_link(totals):
    incoming = prefix_by_axis(totals, NORMAL, compose, identity_map(totals[0]))
    return (incoming[4], incoming[5])


def local(
    state,
    iblank,
    flux,
    left_vectors,
    right_vectors,
    low_one,
    low_two,
    up_one,
    up_two,
    pivot,
    donor_cells,
    donor_weights,
    fringe_cells,
    fringe_live,
):
    current = state[:, 0]
    cell_shape = current.shape
    grids = lax.axis_size("grid")
    mixing = flux[:, :, 0]
    left_local = left_vectors[:, :, 0][:, :, None, :]
    right_local = right_vectors[:, :, 0][:, :, None, :]
    active = iblank[0].astype(jnp.float32)
    corners = donor_cells.reshape(8, -1)
    weights = donor_weights.reshape(8, -1)
    targets = fringe_cells.reshape(-1)
    live_slots = fringe_live.reshape(-1)[None] == 1
    coefficients = (low_one[:, 0], low_two[:, 0], up_one[:, 0], up_two[:, 0], pivot[:, 0])
    for repeat in range(ITERS):
        flat = current.reshape(5, -1)
        picked = jnp.take(flat, corners, axis=1)
        packed = jnp.concatenate([picked, weights[None]], axis=0).reshape(6, 8, grids, -1)
        arrived = lax.all_to_all(packed, "grid", split_axis=2, concat_axis=2, tiled=True).reshape(
            6, 8, -1
        )
        received = jnp.sum(arrived[5:6] * arrived[:5], axis=1)
        existing = jnp.take(flat, targets, axis=1)
        flat = flat.at[:, targets].set(jnp.where(live_slots, received, existing))
        current = flat.reshape(cell_shape)
        padded = extended(current, (("span", 2), (NORMAL, 1)), 2)
        residual = residual_of(padded, mixing)
        source = STEP * small_matrix(left_local, residual)
        lower = linear_pass(coefficients[0], coefficients[1], source, False, forward_link)
        solved = linear_pass(
            coefficients[2], coefficients[3], coefficients[4] * lower, True, backward_link
        )
        change = small_matrix(right_local, solved)
        current = current + active * change
    return current[:, None]


def solution(mesh):
    finer = Mesh(
        mesh.devices.reshape(mesh.shape["grid"], mesh.shape["span"], 8, 2),
        ("grid", "span", "normal_0", "normal_1"),
    )
    in_specs = (
        P(None, "grid", NORMAL, "span"),
        P("grid", NORMAL, "span"),
        P(None, None, "grid"),
        P(None, None, "grid", "span"),
        P(None, None, "grid", "span"),
        P(None, "grid", NORMAL, "span"),
        P(None, "grid", NORMAL, "span"),
        P(None, "grid", NORMAL, "span"),
        P(None, "grid", NORMAL, "span"),
        P(None, "grid", NORMAL, "span"),
        P(None, "grid", NORMAL, "span"),
        P(None, "grid", NORMAL, "span"),
        P("grid", NORMAL, "span"),
        P("grid", NORMAL, "span"),
    )
    out_specs = P(None, "grid", NORMAL, "span")
    return jax.shard_map(local, mesh=finer, in_specs=in_specs, out_specs=out_specs, check_vma=False)
```

profile of v0, /device:TPU:1, one launch (start us, length us, event | category | flops | bytes accessed | tf_op | source)
XLA Modules:
  0.0 767.4 jit_solution(8192990046085050820)
XLA Ops:
  1.9 5.9 copy.145
  7.8 84.9 %gather_fusion = f32[24576,5]{1,0:T(8,128)} fusion(f32[5,16384]{0,1:T(8,128)} %bitcast.719, s32[24576]{0:T(1024)S(1)} %broadcast_clamp_fusion), kind=kCustom, calls=%fused_computation.clone | custom fusion | bytes 1081344 | tf_op jit(solution)/shard_map/jit(_take)/gather | solution.py:209
  92.8 7.7 %copy.146 = f32[8,3072,5]{1,0,2:T(8,128)S(1)} copy(f32[8,3072,5]{2,1,0:T(8,128)} %bitcast.722) | data formatting | bytes 983040 | tf_op jit(solution)/shard_map/jit(_take)/gather | solution.py:209
  115.6 34.1 %scatter_custom_fusion = f32[5,16384]{0,1:T(8,128)} fusion(f32[5,16384]{0,1:T(8,128)} %bitcast.720, s32[3072]{0:T(1024)S(1)} %bitcast.860, f32[5,3072]{0,1:T(8,128)S(1)} %bitcast.724, f32[]{:T(128)} %constant.169.clone.2, pred[3072]{0:T(1024)(128)(4,1)S(1)} %compare_and_fusion.1, pred[3072]{0:T(1024)(128)(4,1)S(1)} %compare_bitcast_fusion, ...), kind=kCustom, calls=%fused_computation.83 | custom fusion | flops 30720 | bytes 2246660 | tf_op jit(solution)/shard_map/scatter | solution.py:216
  149.7 5.7 copy.161
  163.3 5.0 collective-permute-start.2
  189.6 13.7 %while.154 = (s32[]{:T(128)}, f32[5,1024]{1,0:T(8,128)S(1)}, f32[5,1024]{1,0:T(8,128)S(1)}, f32[5,1024]{1,0:T(8,128)S(1)}, f32[5,1024]{1,0:T(8,128)S(1)}, /*inde...) while((s32[]{:T(128)}, f32[5,1024]{1,0:T(8,128)S(1)}, ...), condition=%wide.region_3.6_spmd.clone, body=%wide.region_2.5_spmd.clone.sunk | while | flops 71683 | bytes 606367 | solution.py:161
  203.3 21.6 %all-gather.16 = f32[16,5,1024]{2,1,0:T(8,128)} all-gather(f32[1,5,1024]{2,1,0:T(8,128)S(1)} %bitcast.739), channel_id=2, replica_groups=mesh['grid'=4,'span'=4,'normal_0'=8,'normal_1'=2] {'normal_0','normal_1'}, dimensions={0}, use_global_device_ids=true | all-gather | bytes 348160 | tf_op jit(solution)/shard_map/all_gather | solution.py:17
  224.9 17.3 %all-gather.17 = f32[16,5,1024]{2,1,0:T(8,128)} all-gather(f32[1,5,1024]{2,1,0:T(8,128)S(1)} %bitcast.740), channel_id=3, replica_groups=mesh['grid'=4,'span'=4,'normal_0'=8,'normal_1'=2] {'normal_0','normal_1'}, dimensions={0}, use_global_device_ids=true | all-gather | bytes 348160 | tf_op jit(solution)/shard_map/all_gather | solution.py:17
  242.2 18.6 %all-gather.18 = f32[16,5,1024]{2,1,0:T(8,128)} all-gather(f32[1,5,1024]{2,1,0:T(8,128)S(1)} %bitcast.738), channel_id=4, replica_groups=mesh['grid'=4,'span'=4,'normal_0'=8,'normal_1'=2] {'normal_0','normal_1'}, dimensions={0}, use_global_device_ids=true | all-gather | bytes 348160 | tf_op jit(solution)/shard_map/all_gather | solution.py:17
  260.8 17.3 %all-gather.19 = f32[16,5,1024]{2,1,0:T(8,128)} all-gather(f32[1,5,1024]{2,1,0:T(8,128)S(1)} %bitcast.733), channel_id=5, replica_groups=mesh['grid'=4,'span'=4,'normal_0'=8,'normal_1'=2] {'normal_0','normal_1'}, dimensions={0}, use_global_device_ids=true | all-gather | bytes 348160 | tf_op jit(solution)/shard_map/all_gather | solution.py:17
  278.1 18.6 %all-gather.20 = f32[16,5,1024]{2,1,0:T(8,128)} all-gather(f32[1,5,1024]{2,1,0:T(8,128)S(1)} %bitcast.734), channel_id=6, replica_groups=mesh['grid'=4,'span'=4,'normal_0'=8,'normal_1'=2] {'normal_0','normal_1'}, dimensions={0}, use_global_device_ids=true | all-gather | bytes 348160 | tf_op jit(solution)/shard_map/all_gather | solution.py:17
  296.7 17.3 %all-gather.21 = f32[16,5,1024]{2,1,0:T(8,128)} all-gather(f32[1,5,1024]{2,1,0:T(8,128)S(1)} %bitcast.732), channel_id=7, replica_groups=mesh['grid'=4,'span'=4,'normal_0'=8,'normal_1'=2] {'normal_0','normal_1'}, dimensions={0}, use_global_device_ids=true | all-gather | bytes 348160 | tf_op jit(solution)/shard_map/all_gather | solution.py:17
  317.4 23.2 %while.155 = (s32[]{:T(128)}, f32[5,1024]{1,0:T(8,128)S(1)}, f32[5,1024]{1,0:T(8,128)S(1)}, f32[5,1024]{1,0:T(8,128)S(1)}, f32[5,1024]{1,0:T(8,128)S(1)}, /*inde...) while((s32[]{:T(128)}, f32[5,1024]{1,0:T(8,128)S(1)}, ...), condition=%wide.region_7.10_spmd.clone, body=%wide.region_6.9_spmd.clone.sunk | while | flops 71684 | bytes 553147 | solution.py:161
  343.5 33.3 %all-gather.23 = f32[8,30,1024]{2,1,0:T(8,128)S(1)} all-gather(f32[1,30,1024]{2,1,0:T(8,128)S(1)} %bitcast.745), channel_id=9, replica_groups=mesh['grid'=4,'span'=4,'normal_0'=8,'normal_1'=2] {'normal_0'}, dimensions={0}, use_global_device_ids=true | all-gather | bytes 1105920 | tf_op jit(solution)/shard_map/all_gather | solution.py:42
  380.0 5.3 copy.169
  385.2 84.9 %gather_fusion.1 = f32[24576,5]{1,0:T(8,128)} fusion(f32[5,16384]{0,1:T(8,128)} %copy.169, s32[24576]{0:T(1024)S(1)} %broadcast_clamp_fusion), kind=kCustom, calls=%fused_computation.2.clone | custom fusion | bytes 1081344 | tf_op jit(solution)/shard_map/jit(_take)/gather | solution.py:209
  470.1 7.6 copy.163
  478.2 9.7 %all_to_all.10 = f32[6,8,4,768]{3,1,0,2:T(8,128)S(1)} all-to-all(f32[6,8,4,768]{3,1,0,2:T(8,128)S(1)} %copy.164), channel_id=1, replica_groups=mesh['grid'=4,'span'=4,'normal_0'=8,'normal_1'=2] {'grid'}, dimensions={2} | all-to-all | bytes 1179648 | tf_op jit(solution)/shard_map/all_to_all | solution.py:211
  488.6 34.2 %scatter_custom_fusion.1 = f32[5,16384]{0,1:T(8,128)} fusion(f32[5,16384]{0,1:T(8,128)} %copy.169, s32[3072]{0:T(1024)} %bitcast.861, f32[5,3072]{0,1:T(8,128)S(1)} %bitcast.723, f32[]{:T(128)} %constant.169.clone.2, pred[3072]{0:T(1024)(128)(4,1)S(1)} %copy-done.103, pred[3072]{0:T(1024)(128)(4,1)S(1)} %copy-done.105, s32[3072]{0:T(1024)S(1)} %fusion.118), kind=kCustom, calls=%fused_computation.80 | custom fusion | flops 30720 | bytes 8796672 | tf_op jit(solution)/shard_map/scatter | solution.py:216
  522.8 5.3 copy.176
  534.4 5.3 copy.175
  552.9 8.2 %collective-permute-start.6 = (f32[5,2,1028]{2,1,0:T(2,128)S(1)}, f32[5,2,1028]{2,1,0:T(2,128)S(1)}, u32[]{:S(2)}, u32[]{:S(2)}) collective-permute-start(f32[5,2,1028]{2,1,0:T(2,128)S(1)} %get-tuple-element.1405), channel_id=1, source_target_pairs={{1,0},{2,1},{3,2},{4,3},{5,4},{6,5},{7,6},{8,7},{9,8},{10,9},{11,1... | collective-permute-start | bytes 123368 | tf_op jit(solution)/shard_map/ppermute | solution.py:90
  570.1 28.3 %while.156 = (s32[]{:T(128)}, f32[5,1024]{1,0:T(8,128)S(1)}, f32[5,1024]{1,0:T(8,128)S(1)}, f32[5,1024]{1,0:T(8,128)S(1)}, f32[5,1024]{1,0:T(8,128)S(1)}, /*inde...) while((s32[]{:T(128)}, f32[5,1024]{1,0:T(8,128)S(1)}, ...), condition=%wide.region_11.14_spmd.clone, body=%wide.region_10.13_spmd.clone.sunk | while | flops 71683 | bytes 606367 | solution.py:161
  598.4 17.5 %all-gather.24 = f32[16,5,1024]{2,1,0:T(8,128)S(1)} all-gather(f32[1,5,1024]{2,1,0:T(8,128)S(1)} %bitcast.742), channel_id=10, replica_groups=mesh['grid'=4,'span'=4,'normal_0'=8,'normal_1'=2] {'normal_0','normal_1'}, dimensions={0}, use_global_device_ids=true | all-gather | bytes 348160 | tf_op jit(solution)/shard_map/all_gather | solution.py:17
  615.9 17.5 %all-gather.25 = f32[16,5,1024]{2,1,0:T(8,128)} all-gather(f32[1,5,1024]{2,1,0:T(8,128)S(1)} %bitcast.743), channel_id=11, replica_groups=mesh['grid'=4,'span'=4,'normal_0'=8,'normal_1'=2] {'normal_0','normal_1'}, dimensions={0}, use_global_device_ids=true | all-gather | bytes 348160 | tf_op jit(solution)/shard_map/all_gather | solution.py:17
  633.4 18.6 %all-gather.26 = f32[16,5,1024]{2,1,0:T(8,128)} all-gather(f32[1,5,1024]{2,1,0:T(8,128)S(1)} %bitcast.741), channel_id=12, replica_groups=mesh['grid'=4,'span'=4,'normal_0'=8,'normal_1'=2] {'normal_0','normal_1'}, dimensions={0}, use_global_device_ids=true | all-gather | bytes 348160 | tf_op jit(solution)/shard_map/all_gather | solution.py:17
  652.1 17.3 %all-gather.27 = f32[16,5,1024]{2,1,0:T(8,128)} all-gather(f32[1,5,1024]{2,1,0:T(8,128)S(1)} %bitcast.736), channel_id=13, replica_groups=mesh['grid'=4,'span'=4,'normal_0'=8,'normal_1'=2] {'normal_0','normal_1'}, dimensions={0}, use_global_device_ids=true | all-gather | bytes 348160 | tf_op jit(solution)/shard_map/all_gather | solution.py:17
  669.3 18.6 %all-gather.28 = f32[16,5,1024]{2,1,0:T(8,128)} all-gather(f32[1,5,1024]{2,1,0:T(8,128)S(1)} %bitcast.737), channel_id=14, replica_groups=mesh['grid'=4,'span'=4,'normal_0'=8,'normal_1'=2] {'normal_0','normal_1'}, dimensions={0}, use_global_device_ids=true | all-gather | bytes 348160 | tf_op jit(solution)/shard_map/all_gather | solution.py:17
  687.9 17.3 %all-gather.29 = f32[16,5,1024]{2,1,0:T(8,128)} all-gather(f32[1,5,1024]{2,1,0:T(8,128)S(1)} %bitcast.735), channel_id=15, replica_groups=mesh['grid'=4,'span'=4,'normal_0'=8,'normal_1'=2] {'normal_0','normal_1'}, dimensions={0}, use_global_device_ids=true | all-gather | bytes 348160 | tf_op jit(solution)/shard_map/all_gather | solution.py:17
  706.8 23.0 %while.157 = (s32[]{:T(128)}, f32[5,1024]{1,0:T(8,128)S(1)}, f32[5,1024]{1,0:T(8,128)S(1)}, f32[5,1024]{1,0:T(8,128)S(1)}, f32[5,1024]{1,0:T(8,128)S(1)}, /*inde...) while((s32[]{:T(128)}, f32[5,1024]{1,0:T(8,128)S(1)}, ...), condition=%wide.region_15.18_spmd.clone, body=%wide.region_14.17_spmd.clone.sunk | while | flops 71684 | bytes 553147 | solution.py:161
  732.7 33.1 %all-gather.31 = f32[8,30,1024]{2,1,0:T(8,128)S(1)} all-gather(f32[1,30,1024]{2,1,0:T(8,128)S(1)} %bitcast.747), channel_id=17, replica_groups=mesh['grid'=4,'span'=4,'normal_0'=8,'normal_1'=2] {'normal_0'}, dimensions={0}, use_global_device_ids=true | all-gather | bytes 1105920 | tf_op jit(solution)/shard_map/all_gather | solution.py:42
  (674 shorter events, 176.0 us)
Async XLA Ops:
  1.9 98.6 %copy-start.7 = (pred[8,3072]{1,0:T(8,128)(4,1)}, pred[8,3072]{1,0:T(8,128)(4,1)S(1)}, u32[]{:S(2)}) copy-start(pred[8,3072]{1,0:T(8,128)(4,1)S(1)} %compare_and_fusion) | copy-start | bytes 73732
  101.9 13.0 %all-to-all-start = ((f32[6,8,4,768]{3,1,0,2:T(8,128)}), f32[6,8,4,768]{3,1,0,2:T(8,128)S(1)}, u32[]{:S(2)}, u32[]{:S(2)}) async-start(f32[6,8,4,768]{3,1,0,2:T(8,128)} %copy.147), calls=%async_computation | async-start | bytes 1179648 | tf_op jit(solution)/shard_map/all_to_all | solution.py:211
  106.8 82.1 %copy-start.82 = (f32[1,1,1,1024]{3,2,1,0:T(1,128)}, f32[1,1,1,1024]{3,2,1,0:T(1,128)S(1)}, u32[]{:S(2)}) copy-start(f32[1,1,1,1024]{3,2,1,0:T(1,128)S(1)} %get-tuple-element.1463) | copy-start | bytes 12292
  106.8 82.1 %copy-start.84 = (f32[1,1,1,1024]{3,2,1,0:T(1,128)}, f32[1,1,1,1024]{3,2,1,0:T(1,128)S(1)}, u32[]{:S(2)}) copy-start(f32[1,1,1,1024]{3,2,1,0:T(1,128)S(1)} %get-tuple-element.1464) | copy-start | bytes 12292
  106.9 82.1 %copy-start.86 = (f32[1,1,1,1024]{3,2,1,0:T(1,128)}, f32[1,1,1,1024]{3,2,1,0:T(1,128)S(1)}, u32[]{:S(2)}) copy-start(f32[1,1,1,1024]{3,2,1,0:T(1,128)S(1)} %get-tuple-element.1465) | copy-start | bytes 12292
  106.9 82.1 %copy-start.88 = (f32[1,1,1,1024]{3,2,1,0:T(1,128)}, f32[1,1,1,1024]{3,2,1,0:T(1,128)S(1)}, u32[]{:S(2)}) copy-start(f32[1,1,1,1024]{3,2,1,0:T(1,128)S(1)} %get-tuple-element.1466) | copy-start | bytes 12292
  106.9 82.1 %copy-start.90 = (f32[1,1,1,1024]{3,2,1,0:T(1,128)}, f32[1,1,1,1024]{3,2,1,0:T(1,128)S(1)}, u32[]{:S(2)}) copy-start(f32[1,1,1,1024]{3,2,1,0:T(1,128)S(1)} %get-tuple-element.1467) | copy-start | bytes 12292
  106.9 82.2 %copy-start.68 = (f32[1,1,1,1024]{3,2,1,0:T(1,128)}, f32[1,1,1,1024]{3,2,1,0:T(1,128)S(1)}, u32[]{:S(2)}) copy-start(f32[1,1,1,1024]{3,2,1,0:T(1,128)S(1)} %get-tuple-element.1458) | copy-start | bytes 12292
  106.9 82.2 %copy-start.70 = (f32[1,1,1,1024]{3,2,1,0:T(1,128)}, f32[1,1,1,1024]{3,2,1,0:T(1,128)S(1)}, u32[]{:S(2)}) copy-start(f32[1,1,1,1024]{3,2,1,0:T(1,128)S(1)} %get-tuple-element.1459) | copy-start | bytes 12292
  106.9 82.2 %copy-start.72 = (f32[1,1,1,1024]{3,2,1,0:T(1,128)}, f32[1,1,1,1024]{3,2,1,0:T(1,128)S(1)}, u32[]{:S(2)}) copy-start(f32[1,1,1,1024]{3,2,1,0:T(1,128)S(1)} %get-tuple-element.1460) | copy-start | bytes 12292
  106.9 82.2 %copy-start.74 = (f32[1,1,1,1024]{3,2,1,0:T(1,128)}, f32[1,1,1,1024]{3,2,1,0:T(1,128)S(1)}, u32[]{:S(2)}) copy-start(f32[1,1,1,1024]{3,2,1,0:T(1,128)S(1)} %get-tuple-element.1461) | copy-start | bytes 12292
  106.9 82.2 %copy-start.76 = (f32[1,1,1,1024]{3,2,1,0:T(1,128)}, f32[1,1,1,1024]{3,2,1,0:T(1,128)S(1)}, u32[]{:S(2)}) copy-start(f32[1,1,1,1024]{3,2,1,0:T(1,128)S(1)} %get-tuple-element.1462) | copy-start | bytes 12292
  106.9 82.2 %copy-start.58 = (f32[1,1,1,1024]{3,2,1,0:T(1,128)}, f32[1,1,1,1024]{3,2,1,0:T(1,128)S(1)}, u32[]{:S(2)}) copy-start(f32[1,1,1,1024]{3,2,1,0:T(1,128)S(1)} %get-tuple-element.1453) | copy-start | bytes 12292
  106.9 82.2 %copy-start.60 = (f32[1,1,1,1024]{3,2,1,0:T(1,128)}, f32[1,1,1,1024]{3,2,1,0:T(1,128)S(1)}, u32[]{:S(2)}) copy-start(f32[1,1,1,1024]{3,2,1,0:T(1,128)S(1)} %get-tuple-element.1454) | copy-start | bytes 12292
  107.0 82.2 %copy-start.62 = (f32[1,1,1,1024]{3,2,1,0:T(1,128)}, f32[1,1,1,1024]{3,2,1,0:T(1,128)S(1)}, u32[]{:S(2)}) copy-start(f32[1,1,1,1024]{3,2,1,0:T(1,128)S(1)} %get-tuple-element.1455) | copy-start | bytes 12292
  107.0 82.2 %copy-start.64 = (f32[1,1,1,1024]{3,2,1,0:T(1,128)}, f32[1,1,1,1024]{3,2,1,0:T(1,128)S(1)}, u32[]{:S(2)}) copy-start(f32[1,1,1,1024]{3,2,1,0:T(1,128)S(1)} %get-tuple-element.1456) | copy-start | bytes 12292
  107.0 82.2 %copy-start.66 = (f32[1,1,1,1024]{3,2,1,0:T(1,128)}, f32[1,1,1,1024]{3,2,1,0:T(1,128)S(1)}, u32[]{:S(2)}) copy-start(f32[1,1,1,1024]{3,2,1,0:T(1,128)S(1)} %get-tuple-element.1457) | copy-start | bytes 12292
  107.0 82.3 %copy-start.52 = (f32[1,1,1,1024]{3,2,1,0:T(1,128)}, f32[1,1,1,1024]{3,2,1,0:T(1,128)S(1)}, u32[]{:S(2)}) copy-start(f32[1,1,1,1024]{3,2,1,0:T(1,128)S(1)} %get-tuple-element.1450) | copy-start | bytes 12292
  107.0 82.3 %copy-start.54 = (f32[1,1,1,1024]{3,2,1,0:T(1,128)}, f32[1,1,1,1024]{3,2,1,0:T(1,128)S(1)}, u32[]{:S(2)}) copy-start(f32[1,1,1,1024]{3,2,1,0:T(1,128)S(1)} %get-tuple-element.1451) | copy-start | bytes 12292
  107.0 82.3 %copy-start.56 = (f32[1,1,1,1024]{3,2,1,0:T(1,128)}, f32[1,1,1,1024]{3,2,1,0:T(1,128)S(1)}, u32[]{:S(2)}) copy-start(f32[1,1,1,1024]{3,2,1,0:T(1,128)S(1)} %get-tuple-element.1452) | copy-start | bytes 12292
  107.1 82.2 %copy-start.78 = (f32[1,1,1,1024]{3,2,1,0:T(1,128)}, f32[1,1,1,1024]{3,2,1,0:T(1,128)S(1)}, u32[]{:S(2)}) copy-start(f32[1,1,1,1024]{3,2,1,0:T(1,128)S(1)} %get-tuple-element.1469) | copy-start | bytes 12292
  107.1 82.2 %copy-start.80 = (f32[1,1,1,1024]{3,2,1,0:T(1,128)}, f32[1,1,1,1024]{3,2,1,0:T(1,128)S(1)}, u32[]{:S(2)}) copy-start(f32[1,1,1,1024]{3,2,1,0:T(1,128)S(1)} %get-tuple-element.1474) | copy-start | bytes 12292
  155.7 6.9 collective-permute-start
  157.0 6.1 collective-permute-start.1
  163.3 24.6 %collective-permute-start.2 = (f32[5,2,1028]{2,1,0:T(2,128)S(1)}, f32[5,2,1028]{2,1,0:T(2,128)S(1)}, u32[]{:S(2)}, u32[]{:S(2)}) collective-permute-start(f32[5,2,1028]{2,1,0:T(2,128)S(1)} %get-tuple-element.1407), channel_id=1, source_target_pairs={{1,0},{2,1},{3,2},{4,3},{5,4},{6,5},{7,6},{8,7},{9,8},{10,9},{11,1... | collective-permute-start | bytes 123368 | tf_op jit(solution)/shard_map/ppermute | solution.py:90
  168.3 19.6 %collective-permute-start.3 = (f32[5,2,1028]{2,1,0:T(2,128)S(1)}, f32[5,2,1028]{2,1,0:T(2,128)S(1)}, u32[]{:S(2)}, u32[]{:S(2)}) collective-permute-start(f32[5,2,1028]{2,1,0:T(2,128)S(1)} %get-tuple-element.1408), channel_id=1, source_target_pairs={{0,1},{1,2},{2,3},{3,4},{4,5},{5,6},{6,7},{7,8},{8,9},{9,10},{10,1... | collective-permute-start | bytes 123368 | tf_op jit(solution)/shard_map/ppermute | solution.py:89
  385.2 92.4 %copy-start.8 = (pred[8,3072]{1,0:T(8,128)(4,1)S(1)}, pred[8,3072]{1,0:T(8,128)(4,1)}, u32[]{:S(2)}) copy-start(pred[8,3072]{1,0:T(8,128)(4,1)} %copy-done.7) | copy-start | bytes 73732
  528.4 11.2 %collective-permute-start.4 = (f32[5,16,2]{2,1,0:T(8,128)S(1)}, f32[5,16,2]{2,1,0:T(8,128)S(1)}, u32[]{:S(2)}, u32[]{:S(2)}) collective-permute-start(f32[5,16,2]{2,1,0:T(8,128)S(1)} %get-tuple-element.1409), channel_id=1, source_target_pairs={{16,0},{32,16},{48,32},{17,1},{33,17},{49,33},{18,2},{34,18},{50,3... | collective-permute-start | bytes 1928 | tf_op jit(solution)/shard_map/ppermute | solution.py:90
  529.7 9.9 %collective-permute-start.5 = (f32[5,16,2]{2,1,0:T(8,128)S(1)}, f32[5,16,2]{2,1,0:T(8,128)S(1)}, u32[]{:S(2)}, u32[]{:S(2)}) collective-permute-start(f32[5,16,2]{2,1,0:T(8,128)S(1)} %get-tuple-element.1410), channel_id=1, source_target_pairs={{0,16},{16,32},{32,48},{1,17},{17,33},{33,49},{2,18},{18,34},{34,5... | collective-permute-start | bytes 1928 | tf_op jit(solution)/shard_map/ppermute | solution.py:89
  546.2 160.1 %copy-start = (f32[5,1,16,1024]{3,2,1,0:T(8,128)S(1)}, f32[5,1,16,1024]{3,2,1,0:T(8,128)}, u32[]{:S(2)}) copy-start(f32[5,1,16,1024]{3,2,1,0:T(8,128)} %param.39) | copy-start | bytes 983044
  552.9 14.8 %collective-permute-start.6 = (f32[5,2,1028]{2,1,0:T(2,128)S(1)}, f32[5,2,1028]{2,1,0:T(2,128)S(1)}, u32[]{:S(2)}, u32[]{:S(2)}) collective-permute-start(f32[5,2,1028]{2,1,0:T(2,128)S(1)} %get-tuple-element.1405), channel_id=1, source_target_pairs={{1,0},{2,1},{3,2},{4,3},{5,4},{6,5},{7,6},{8,7},{9,8},{10,9},{11,1... | collective-permute-start | bytes 123368 | tf_op jit(solution)/shard_map/ppermute | solution.py:90
  561.1 6.6 collective-permute-start.7
  (86 other events, 4187.2 us)
where the time goes:
time: 780 us; the launch traced here: 767 us
  blocking collectives  297 us (38%)
  local copies, waits for them, and re-layouts  258 us (33%)
  other arithmetic  167 us (21%)
  starting transfers between devices  37 us (5%)
    all_gather x12, blocking collectives, carried_in(): gathered = jax.tree.map(lambda a: lax.all_gather(a, axis), part)  217 us
    gather x4, local copies, waits for them, and re-layouts, local(): picked = jnp.take(flat, corners, axis=1)  185 us
    all_gather x4, blocking collectives, gathered_once(): both, at, found = (lax.all_gather(jnp.concatenate(lines), axis), 0, {})  70.4 us
    scatter x2, other arithmetic, local(): flat = flat.at[:, targets].set(jnp.where(live_slots, received, existing))  68.3 us
    unnamed x38, other arithmetic  28.2 us
    sub x32, other arithmetic, advance(): two_next = -coef_one * two_now - coef_two * two_prev  26.5 us
    dynamic_update_slice x32, other arithmetic, linear_pass(): final, outputs = lax.scan(advance, start, moved, reverse=reverse)  25.9 us
    dynamic_update_slice x192, local copies, waits for them, and re-layouts, linear_pass(): final, outputs = lax.scan(advance, start, moved, reverse=reverse)  17.5 us
  transfers between devices with their start and end apart: 9, of which 2 were waited for; matrix products, arithmetic and copies ran while one was open for 4% of the time, Pallas kernels for 0%

commit v1 on v0

v1 whole, which is shorter than its diff:
```python
import jax
import jax.numpy as jnp
from jax import lax
from jax.experimental import pallas as pl
from jax.experimental.pallas import tpu as pltpu
from jax.sharding import PartitionSpec as P

ITERS = 2
GRIDS = 4
SPANS = 4
NORMALS = 16
CAP = 6
ROWS = 16
COMP = 5
LINE = 40
ORDER = (2, 1, 3)
F32, BF16 = jnp.float32, jnp.bfloat16
LANE_GATHER = lax.GatherDimensionNumbers(
    offset_dims=(),
    collapsed_slice_dims=(1,),
    start_index_map=(1,),
    operand_batching_dims=(0,),
    start_indices_batching_dims=(0,),
)


def lane_gather(table, index):
    return lax.gather(
        table,
        index[:, :, None],
        LANE_GATHER,
        slice_sizes=(1, 1),
        mode=lax.GatherScatterMode.PROMISE_IN_BOUNDS,
    )


def iota(shape, dim):
    return lax.broadcasted_iota(jnp.int32, shape, dim)


def to_lines(raw, lines):
    for c in range(COMP):
        for half in range(2):
            for a in range(8):
                tile = raw[c, half * 8 : half * 8 + 8, a * 128 : a * 128 + 128]
                lines[pl.ds(half * 8 * LINE + c * 8 + a, 8, stride=LINE), :] = tile


def kernel(
    state,
    iblank,
    flux,
    left,
    right,
    low_one,
    low_two,
    up_one,
    up_two,
    pivot,
    donor_cells,
    donor_weights,
    fringe_cells,
    fringe_live,
    out,
    raw,
    iblank_v,
    flux_v,
    left_v,
    right_v,
    cells_v,
    weights_v,
    fringe_v,
    live_v,
    cur,
    low1,
    low2,
    up1,
    up2,
    piv,
    active,
    mix_c,
    mix_d,
    src,
    one_rows,
    two_rows,
    table,
    onehots,
    inverse,
    inv_row,
    inv_lane,
    sent,
    received,
    ysend,
    yrecv,
    halo_l,
    halo_r,
    zlo,
    zhi,
    mats,
    mats_in,
    bounds,
    bounds_in,
    enter_out,
    enter,
    in_sem,
    slot_ssem,
    slot_rsem,
    y_ssem,
    y_rsem,
    z_ssem,
    z_rsem,
    mat_ssem,
    mat_rsem,
    b_ssem,
    b_rsem,
    e_ssem,
    e_rsem,
):
    g = lax.axis_index("grid")
    s = lax.axis_index("span")
    n = lax.axis_index("normal")
    leader = jnp.logical_and(lax.rem(n, 3) == 0, n < 15)
    comp_me = lax.div(n, 3)

    pairs = [
        (state, raw.at[0]),
        (donor_cells, cells_v),
        (donor_weights, weights_v),
        (low_one, raw.at[1]),
        (low_two, raw.at[2]),
        (up_one, raw.at[3]),
        (up_two, raw.at[4]),
        (pivot, raw.at[5]),
        (fringe_cells, fringe_v),
        (fringe_live, live_v),
        (left, left_v),
        (flux, flux_v),
        (right, right_v),
        (iblank, iblank_v),
    ]
    loads = [pltpu.make_async_copy(a, b, in_sem.at[k]) for k, (a, b) in enumerate(pairs)]
    for load in loads:
        load.start()

    barrier = pltpu.get_barrier_semaphore()
    for k in range(1, GRIDS):
        pl.semaphore_signal(barrier, inc=1, device_id={"grid": lax.rem(g + k, GRIDS)})
    for k in range(1, NORMALS):
        pl.semaphore_signal(barrier, inc=1, device_id={"normal": lax.rem(n + k, NORMALS)})

    for k in (1, SPANS - 1):
        pl.semaphore_signal(barrier, inc=1, device_id={"span": lax.rem(s + k, SPANS)})

    def barrier_wait():
        pl.semaphore_wait(barrier, GRIDS - 1 + NORMALS - 1 + 2)

    zeros8 = jnp.zeros((8, 128), F32)

    @pl.when(s == 0)
    def _():
        for it in range(ITERS):
            yrecv[it, 0] = zeros8

    @pl.when(s == SPANS - 1)
    def _():
        for it in range(ITERS):
            yrecv[it, 1] = zeros8

    @pl.when(n == 0)
    def _():
        for it in range(ITERS):
            zlo[it] = jnp.zeros((2 * LINE, 128), F32)

    @pl.when(n == NORMALS - 1)
    def _():
        for it in range(ITERS):
            zhi[it] = jnp.zeros((2 * LINE, 128), F32)

    loads[0].wait()
    to_lines(raw.at[0], cur)
    loads[1].wait()
    loads[2].wait()

    def slot_copy(it, k):
        return pltpu.make_async_remote_copy(
            src_ref=sent.at[it, k - 1],
            dst_ref=received.at[it, k - 1],
            send_sem=slot_ssem.at[it, k - 1],
            recv_sem=slot_rsem.at[it, k - 1],
            device_id={"grid": lax.rem(g + k, GRIDS)},
            device_id_type=pl.DeviceIdType.MESH,
        )

    def y_copy(it, side):
        return pltpu.make_async_remote_copy(
            src_ref=ysend.at[it, side],
            dst_ref=yrecv.at[it, side],
            send_sem=y_ssem.at[it, side],
            recv_sem=y_rsem.at[it, side],
            device_id={"span": s + (1 if side == 0 else -1)},
            device_id_type=pl.DeviceIdType.MESH,
        )

    def z_copy(it, side):
        return pltpu.make_async_remote_copy(
            src_ref=cur.at[pl.ds((ROWS - 2) * LINE if side == 0 else 0, 2 * LINE), :],
            dst_ref=(zlo if side == 0 else zhi).at[it],
            send_sem=z_ssem.at[it, side],
            recv_sem=z_rsem.at[it, side],
            device_id={"normal": n + (1 if side == 0 else -1)},
            device_id_type=pl.DeviceIdType.MESH,
        )

    def mat_copy(c):
        return pltpu.make_async_remote_copy(
            src_ref=mats.at[c],
            dst_ref=mats_in.at[n],
            send_sem=mat_ssem.at[c],
            recv_sem=mat_rsem.at[n],
            device_id={"normal": 3 * c},
            device_id_type=pl.DeviceIdType.MESH,
        )

    def b_copy(it, c):
        return pltpu.make_async_remote_copy(
            src_ref=bounds.at[it, c],
            dst_ref=bounds_in.at[it, n],
            send_sem=b_ssem.at[it, c],
            recv_sem=b_rsem.at[it, n],
            device_id={"normal": 3 * c},
            device_id_type=pl.DeviceIdType.MESH,
        )

    def b_arrival(it, k):
        return pltpu.make_async_remote_copy(
            src_ref=bounds.at[it, 0],
            dst_ref=bounds_in.at[it, k],
            send_sem=b_ssem.at[it, 0],
            recv_sem=b_rsem.at[it, k],
            device_id={"normal": k},
            device_id_type=pl.DeviceIdType.MESH,
        )

    def mat_arrival(k):
        return pltpu.make_async_remote_copy(
            src_ref=mats.at[0],
            dst_ref=mats_in.at[k],
            send_sem=mat_ssem.at[0],
            recv_sem=mat_rsem.at[k],
            device_id={"normal": k},
            device_id_type=pl.DeviceIdType.MESH,
        )

    def e_copy(it, k):
        return pltpu.make_async_remote_copy(
            src_ref=enter_out.at[it, k],
            dst_ref=enter.at[it, comp_me],
            send_sem=e_ssem.at[it, k],
            recv_sem=e_rsem.at[it, comp_me],
            device_id={"normal": k},
            device_id_type=pl.DeviceIdType.MESH,
        )

    def e_arrival(it, c):
        return pltpu.make_async_remote_copy(
            src_ref=enter_out.at[it, 0],
            dst_ref=enter.at[it, c],
            send_sem=e_ssem.at[it, 0],
            recv_sem=e_rsem.at[it, c],
            device_id={"normal": 3 * c},
            device_id_type=pl.DeviceIdType.MESH,
        )

    def interpolate(it):
        for c in range(COMP):
            for m in range(0, 8, 2):
                for p in range(2):
                    x = jnp.concatenate(
                        [
                            cur[(2 * m + p) * LINE + c * 8 : (2 * m + p) * LINE + c * 8 + 8, :],
                            cur[(2 * m + 2 + p) * LINE + c * 8 : (2 * m + 2 + p) * LINE + c * 8 + 8, :],
                        ],
                        axis=0,
                    )
                    head = x.astype(BF16)
                    tail = (x - head.astype(F32)).astype(BF16)
                    rows = slice(c * 64 + m * 8, c * 64 + m * 8 + 16)
                    table[rows, p * 128 : p * 128 + 128] = head
                    table[rows, 256 + p * 128 : 256 + p * 128 + 128] = tail
        for turn, k in enumerate(ORDER):
            receiver = lax.rem(g + k, GRIDS)

            def one_row(b, _, k=k, receiver=receiver):
                row = receiver * CAP + b
                total = [zeros8] * COMP
                for pair in range(4):
                    cells = [cells_v[2 * pair + e, pl.ds(row, 1), :] for e in range(2)]
                    if it == 0:
                        parts = []
                        for cell in cells:
                            low = ((cell >> 10) & 1) * 128 + (cell & 127)
                            low = jnp.broadcast_to(low.astype(F32).astype(BF16), (256, 128))
                            rank = iota((256, 128), 0).astype(F32).astype(BF16)
                            parts.append(
                                jnp.where(rank == low, jnp.ones((), BF16), jnp.zeros((), BF16))
                            )
                        hot = jnp.concatenate(parts, axis=1)
                        onehots[((k - 1) * CAP + b) * 4 + pair] = hot
                    else:
                        hot = onehots[((k - 1) * CAP + b) * 4 + pair]
                    found = jnp.dot(
                        table[...],
                        jnp.concatenate([hot, hot], axis=0),
                        preferred_element_type=F32,
                    )
                    for e in range(2):
                        high = ((cells[e] >> 11) << 3) | ((cells[e] >> 7) & 7)
                        weight = jnp.broadcast_to(
                            weights_v[2 * pair + e, pl.ds(row, 1), :], (8, 128)
                        )
                        for v in range(8):
                            mask = jnp.where(iota((8, 128), 0) + v * 8 == high, weight, 0.0)
                            for c in range(COMP):
                                at = c * 64 + v * 8
                                total[c] = (
                                    total[c] + found[at : at + 8, e * 128 : e * 128 + 128] * mask
                                )
                for c in range(COMP):
                    sent[it, k - 1, pl.ds(b * COMP + c, 1), :] = jnp.sum(
                        total[c], axis=0, keepdims=True
                    )
                return 0

            lax.fori_loop(0, CAP, one_row, 0)
            if it == 0 and turn == 0:
                barrier_wait()
            slot_copy(it, k).start()

    def invert_fringe():
        inverse[...] = jnp.zeros((256, 128), F32)
        for k in ORDER:
            source = lax.rem(g + GRIDS - k, GRIDS)

            def one(b, _, k=k, source=source):
                row = source * CAP + b
                cell = fringe_v[pl.ds(row, 1), :]
                live = live_v[pl.ds(row, 1), :]
                high = jnp.where(live == 1, cell >> 7, -1)
                low = cell & 127
                number = (((k - 1) * CAP + b) + 1).astype(F32)
                at = jnp.where(iota((128, 128), 0) == high, 1.0, 0.0)
                lane = iota((128, 128), 1).astype(F32)
                a = jnp.concatenate([at * number, at * lane], axis=0).astype(BF16)
                col = jnp.where(iota((128, 128), 0) == low, 1.0, 0.0).astype(BF16)
                inverse[...] += lax.dot_general(
                    a, col, (((1,), (1,)), ((), ())), preferred_element_type=F32
                )
                return 0

            lax.fori_loop(0, CAP, one, 0)
        inv_row[...] = inverse[0:128, :].astype(jnp.int32) - 1
        inv_lane[...] = inverse[128:256, :].astype(jnp.int32)

    def line(ref, i):
        return ref[i * LINE : i * LINE + LINE, :]

    def block_matrices():
        zero = jnp.zeros((LINE, 128), F32)
        ones = jnp.ones((LINE, 128), F32)
        a1, a2, b1, b2 = ones, zero, zero, ones
        for i in range(ROWS):
            c1, c2 = line(low1, i), line(low2, i)
            a1, a2 = -c1 * a1 - c2 * a2, a1
            b1, b2 = -c1 * b1 - c2 * b2, b1
            one_rows[i * LINE : i * LINE + LINE, :] = a1
            two_rows[i * LINE : i * LINE + LINE, :] = b1
        found = [a1, b1, a2, b2]
        a1, a2, b1, b2 = ones, zero, zero, ones
        p1 = p2 = q1 = q2 = zero
        for i in reversed(range(ROWS)):
            c1, c2, pv = line(up1, i), line(up2, i), line(piv, i)
            a1, a2 = -c1 * a1 - c2 * a2, a1
            b1, b2 = -c1 * b1 - c2 * b2, b1
            p1, p2 = pv * line(one_rows, i) - c1 * p1 - c2 * p2, p1
            q1, q2 = pv * line(two_rows, i) - c1 * q1 - c2 * q2, q1
        found += [a1, b1, a2, b2, p1, q1, p2, q2]
        for c in range(COMP):
            for j, whole in enumerate(found):
                mats[c, j] = whole[c * 8 : c * 8 + 8, :]

    def prepare():
        for k, lines in ((3, low1), (4, low2), (5, up1), (6, up2), (7, piv)):
            loads[k].wait()
            to_lines(raw.at[k - 2], lines)
        block_matrices()
        for c in range(COMP):

            @pl.when(n != 3 * c)
            def _(c=c):
                mat_copy(c).start()

        @pl.when(leader)
        def _():
            mats_in[n] = mats[comp_me]

        loads[8].wait()
        loads[9].wait()
        invert_fringe()

    def prepare_mixing():
        loads[10].wait()
        loads[11].wait()
        f = [[jnp.broadcast_to(flux_v[k, m : m + 1].reshape(1, 1), (8, 128)) for m in range(COMP)] for k in range(COMP)]
        for c in range(COMP):
            row = [left_v[c * COMP + k] for k in range(COMP)]
            for m in range(COMP):
                total = row[0] * f[0][m]
                for k in range(1, COMP):
                    total = total + row[k] * f[k][m]
                mix_c[c * COMP + m] = total * -0.2
                mix_d[c * COMP + m] = row[m] * -0.024

    def place_rows(it, k, i_list):
        for i in i_list:
            lanes = inv_lane[i * 8 : i * 8 + 8, :]
            rows = inv_row[i * 8 : i * 8 + 8, :]
            values = [cur[i * LINE + c * 8 : i * LINE + c * 8 + 8, :] for c in range(COMP)]
            for b in range(CAP):
                hit = rows == (k - 1) * CAP + b
                for c in range(COMP):
                    slots = received[it, k - 1, pl.ds(b * COMP + c, 8, stride=0), :]
                    values[c] = jnp.where(hit, lane_gather(slots, lanes), values[c])
            for c in range(COMP):
                cur[i * LINE + c * 8 : i * LINE + c * 8 + 8, :] = values[c]

    def place(it):
        for turn, k in enumerate(ORDER):
            slot_copy(it, k).wait_recv()
            if turn == GRIDS - 2:
                place_rows(it, k, (0, 1, 14, 15))
                start_z(it)
                place_rows(it, k, range(2, 14))
            else:
                place_rows(it, k, range(ROWS))

    def start_z(it):
        @pl.when(n < NORMALS - 1)
        def _():
            z_copy(it, 0).start()

        @pl.when(n > 0)
        def _():
            z_copy(it, 1).start()

    def start_y(it):
        lane = iota((8, 128), 1)
        for side in range(2):
            total = zeros8
            for m in range(10):
                rows = cur[pl.ds(m * 64 + (7 if side == 0 else 0), 8, stride=8), :]
                shift = (2 * m + (2 if side == 0 else 0)) % 128
                rows = pltpu.roll(rows, shift, 1) if shift else rows
                total = jnp.where((lane >> 1) == m, rows, total)
            ysend[it, side] = total

        @pl.when(s < SPANS - 1)
        def _():
            y_copy(it, 0).start()

        @pl.when(s > 0)
        def _():
            y_copy(it, 1).start()

    def finish_y(it):
        @pl.when(s > 0)
        def _():
            y_copy(it, 0).wait_recv()

        @pl.when(s < SPANS - 1)
        def _():
            y_copy(it, 1).wait_recv()

        for side, halo in ((0, halo_l), (1, halo_r)):
            packed = yrecv[it, side]
            for m in range(10):
                shift = (126 - 2 * m) if side == 0 else (128 - 2 * m) % 128
                halo[m * 8 : m * 8 + 8, :] = pltpu.roll(packed, shift, 1) if shift else packed

    def source_row(it, i):
        lane = iota((8, 128), 1)
        sub = iota((8, 128), 0)

        def at(row, c):
            if row < 0:
                return zlo[it, (row + 2) * LINE + c * 8 : (row + 2) * LINE + c * 8 + 8, :]
            if row >= ROWS:
                return zhi[it, (row - ROWS) * LINE + c * 8 : (row - ROWS) * LINE + c * 8 + 8, :]
            return cur[row * LINE + c * 8 : row * LINE + c * 8 + 8, :]

        central, fourth = [], []
        for c in range(COMP):
            x = at(i, c)
            above = jnp.where(
                sub == 7, halo_r[pl.ds(i * COMP + c, 8, stride=0), :], pltpu.roll(x, 7, 0)
            )
            below = jnp.where(
                sub == 0, halo_l[pl.ds(i * COMP + c, 8, stride=0), :], pltpu.roll(x, 1, 0)
            )
            plus1 = pltpu.roll(jnp.where(lane < 1, above, x), 127, 1)
            plus2 = pltpu.roll(jnp.where(lane < 2, above, x), 126, 1)
            minus1 = pltpu.roll(jnp.where(lane >= 127, below, x), 1, 1)
            minus2 = pltpu.roll(jnp.where(lane >= 126, below, x), 2, 1)
            central.append(plus1 - minus1)
            near = (plus1 + minus1) + (at(i + 1, c) + at(i - 1, c))
            far = (plus2 + minus2) + (at(i + 2, c) + at(i - 2, c))
            fourth.append(far - 4.0 * near + 12.0 * x)
        for c in range(COMP):
            total = mix_c[c * COMP] * central[0] + mix_d[c * COMP] * fourth[0]
            for m in range(1, COMP):
                total = total + mix_c[c * COMP + m] * central[m] + mix_d[c * COMP + m] * fourth[m]
            src[i * LINE + c * 8 : i * LINE + c * 8 + 8, :] = total

    def sweep(e1, e2, f1, f2):
        for i in range(ROWS):
            e1, e2 = line(src, i) - line(low1, i) * e1 - line(low2, i) * e2, e1
            one_rows[i * LINE : i * LINE + LINE, :] = e1
        for i in reversed(range(ROWS)):
            f1, f2 = line(piv, i) * line(one_rows, i) - line(up1, i) * f1 - line(up2, i) * f2, f1
            two_rows[i * LINE : i * LINE + LINE, :] = f1
        return e1, e2, f1, f2

    def lead(it):
        def arrive(k, _):
            @pl.when(k != n)
            def _():
                if it == 0:
                    mat_arrival(k).wait_recv()
                b_arrival(it, k).wait_recv()

            return 0

        lax.fori_loop(0, NORMALS, arrive, 0)
        e1 = e2 = zeros8
        pushed = []
        for k in range(NORMALS):
            enter_out[it, k, 0] = e1
            enter_out[it, k, 1] = e2
            pushed.append(
                (
                    mats_in[k, 8] * e1 + mats_in[k, 9] * e2 + bounds_in[it, k, 2],
                    mats_in[k, 10] * e1 + mats_in[k, 11] * e2 + bounds_in[it, k, 3],
                )
            )
            e1, e2 = (
                mats_in[k, 0] * e1 + mats_in[k, 1] * e2 + bounds_in[it, k, 0],
                mats_in[k, 2] * e1 + mats_in[k, 3] * e2 + bounds_in[it, k, 1],
            )
        f1 = f2 = zeros8
        for k in reversed(range(NORMALS)):
            enter_out[it, k, 2] = f1
            enter_out[it, k, 3] = f2
            f1, f2 = (
                mats_in[k, 4] * f1 + mats_in[k, 5] * f2 + pushed[k][0],
                mats_in[k, 6] * f1 + mats_in[k, 7] * f2 + pushed[k][1],
            )
        for far in range(8, 0, -1):
            for off in {far, NORMALS - far}:
                e_copy(it, lax.rem(n + off, NORMALS)).start()
        enter[it, comp_me] = enter_out[it, n]

    def lines_step(it):
        zero = jnp.zeros((LINE, 128), F32)
        found = sweep(zero, zero, zero, zero)
        for c in range(COMP):
            for j, whole in enumerate(found):
                bounds[it, c, j] = whole[c * 8 : c * 8 + 8, :]
        for c in range(COMP):

            @pl.when(n != 3 * c)
            def _(c=c):
                b_copy(it, c).start()

        @pl.when(leader)
        def _():
            bounds_in[it, n] = bounds[it, comp_me]
            lead(it)

        if it == 0:
            finish_loads()
        for c in range(COMP):

            @pl.when(n != 3 * c)
            def _(c=c):
                e_arrival(it, c).wait_recv()

        entering = [
            jnp.concatenate([enter[it, c, j] for c in range(COMP)], axis=0) for j in range(4)
        ]
        sweep(*entering)

    def finish_loads():
        loads[12].wait()
        loads[13].wait()
        for half in range(2):
            for a in range(8):
                tile = iblank_v[half * 8 : half * 8 + 8, a * 128 : a * 128 + 128]
                active[pl.ds(half * 64 + a, 8, stride=8), :] = tile.astype(F32)

    def update(it):
        for i in range(ROWS):
            solved = [two_rows[i * LINE + m * 8 : i * LINE + m * 8 + 8, :] for m in range(COMP)]
            mask = active[i * 8 : i * 8 + 8, :]
            for c in range(COMP):
                total = right_v[c * COMP] * solved[0]
                for m in range(1, COMP):
                    total = total + right_v[c * COMP + m] * solved[m]
                at = slice(i * LINE + c * 8, i * LINE + c * 8 + 8)
                cur[at, :] = cur[at, :] + mask * total

    for it in range(ITERS):
        interpolate(it)
        if it == 0:
            prepare()
            prepare_mixing()
        place(it)
        start_y(it)
        finish_y(it)
        for i in range(2, ROWS - 2):
            source_row(it, i)

        @pl.when(n > 0)
        def _(it=it):
            z_copy(it, 0).wait_recv()

        @pl.when(n < NORMALS - 1)
        def _(it=it):
            z_copy(it, 1).wait_recv()

        for i in (0, 1, ROWS - 2, ROWS - 1):
            source_row(it, i)
        lines_step(it)

        @pl.when(n < NORMALS - 1)
        def _(it=it):
            z_copy(it, 0).wait_send()

        @pl.when(n > 0)
        def _(it=it):
            z_copy(it, 1).wait_send()

        update(it)

    for c in range(COMP):
        for half in range(2):
            for a in range(8):
                out[c, half * 8 : half * 8 + 8, a * 128 : a * 128 + 128] = cur[
                    pl.ds(half * 8 * LINE + c * 8 + a, 8, stride=LINE), :
                ]

    for it in range(ITERS):
        for k in ORDER:
            slot_copy(it, k).wait_send()

        @pl.when(s < SPANS - 1)
        def _(it=it):
            y_copy(it, 0).wait_send()

        @pl.when(s > 0)
        def _(it=it):
            y_copy(it, 1).wait_send()

        for c in range(COMP):

            @pl.when(n != 3 * c)
            def _(c=c, it=it):
                if it == 0:
                    mat_copy(c).wait_send()
                b_copy(it, c).wait_send()

        @pl.when(leader)
        def _(it=it):
            for off in range(1, NORMALS):
                e_copy(it, lax.rem(n + off, NORMALS)).wait_send()


def vmem(*shape, dtype=F32):
    return pltpu.VMEM(shape, dtype)


def local(
    state,
    iblank,
    flux,
    left_vectors,
    right_vectors,
    low_one,
    low_two,
    up_one,
    up_two,
    pivot,
    donor_cells,
    donor_weights,
    fringe_cells,
    fringe_live,
):
    dma = pltpu.SemaphoreType.DMA
    whole = ROWS * LINE
    slots = GRIDS * CAP
    out = pl.pallas_call(
        kernel,
        out_shape=jax.ShapeDtypeStruct((COMP, ROWS, 1024), F32),
        in_specs=[pl.BlockSpec(memory_space=pltpu.HBM)] * 14,
        out_specs=pl.BlockSpec(memory_space=pltpu.VMEM),
        scratch_shapes=[
            vmem(6, COMP, ROWS, 1024),
            vmem(ROWS, 1024, dtype=jnp.int32),
            vmem(COMP, COMP),
            vmem(25, 8, 128),
            vmem(25, 8, 128),
            vmem(8, slots, 128, dtype=jnp.int32),
            vmem(8, slots, 128),
            vmem(slots, 128, dtype=jnp.int32),
            vmem(slots, 128, dtype=jnp.int32),
            vmem(whole, 128),
            vmem(whole, 128),
            vmem(whole, 128),
            vmem(whole, 128),
            vmem(whole, 128),
            vmem(whole, 128),
            vmem(ROWS * 8, 128),
            vmem(25, 8, 128),
            vmem(25, 8, 128),
            vmem(whole, 128),
            vmem(whole, 128),
            vmem(whole, 128),
            vmem(320, 512, dtype=BF16),
            vmem(72, 256, 256, dtype=BF16),
            vmem(256, 128),
            vmem(128, 128, dtype=jnp.int32),
            vmem(128, 128, dtype=jnp.int32),
            vmem(ITERS, 3, CAP * COMP, 128),
            vmem(ITERS, 3, CAP * COMP, 128),
            vmem(ITERS, 2, 8, 128),
            vmem(ITERS, 2, 8, 128),
            vmem(80, 128),
            vmem(80, 128),
            vmem(ITERS, 2 * LINE, 128),
            vmem(ITERS, 2 * LINE, 128),
            vmem(COMP, 12, 8, 128),
            vmem(NORMALS, 12, 8, 128),
            vmem(ITERS, COMP, 4, 8, 128),
            vmem(ITERS, NORMALS, 4, 8, 128),
            vmem(ITERS, NORMALS, 4, 8, 128),
            vmem(ITERS, COMP, 4, 8, 128),
            dma((14,)),
            dma((ITERS, 3)),
            dma((ITERS, 3)),
            dma((ITERS, 2)),
            dma((ITERS, 2)),
            dma((ITERS, 2)),
            dma((ITERS, 2)),
            dma((COMP,)),
            dma((NORMALS,)),
            dma((ITERS, COMP)),
            dma((ITERS, NORMALS)),
            dma((ITERS, NORMALS)),
            dma((ITERS, COMP)),
        ],
        compiler_params=pltpu.CompilerParams(
            collective_id=0, has_side_effects=True, vmem_limit_bytes=48 << 20
        ),
        name="adi_window",
    )(
        state[:, 0],
        iblank[0],
        flux[:, :, 0],
        left_vectors.reshape(25, 8, 128),
        right_vectors.reshape(25, 8, 128),
        low_one[:, 0],
        low_two[:, 0],
        up_one[:, 0],
        up_two[:, 0],
        pivot[:, 0],
        donor_cells[:, 0],
        donor_weights[:, 0],
        fringe_cells[0],
        fringe_live[0],
    )
    return out[:, None]


def solution(mesh):
    cells = P(None, "grid", "normal", "span")
    slots = P("grid", "normal", "span")
    lines = P(None, None, "grid", "span")
    return jax.shard_map(
        local,
        mesh=mesh,
        in_specs=(
            cells,
            slots,
            P(None, None, "grid"),
            lines,
            lines,
            cells,
            cells,
            cells,
            cells,
            cells,
            cells,
            cells,
            slots,
            slots,
        ),
        out_specs=cells,
        check_vma=False,
    )
```

time: 780 us -> 78.7 us (0.10); the launches traced: 767 us -> 78.2 us
  blocking collectives: 297 us -> 0 us
  local copies, waits for them, and re-layouts: 258 us -> 11.7 us
  other arithmetic: 167 us -> 0 us
  Pallas kernels: 0 us -> 66.5 us
  starting transfers between devices: 37 us -> 0 us
    all_gather x16 -> x0, blocking collectives: 288 us -> none  [the longest x12 217 us: carried_in(): gathered = jax.tree.map(lambda a: lax.all_gather(a, axis), part)]
    gather x4 -> x0, local copies, waits for them, and re-layouts: 185 us -> none  [local(): picked = jnp.take(flat, corners, axis=1)]
    scatter x2 -> x0, other arithmetic: 68.3 us -> none  [local(): flat = flat.at[:, targets].set(jnp.where(live_slots, received, existing))]
    pallas_call x0 -> x1, Pallas kernels: none -> 66.5 us  [local(): pl.pallas_call(kernel, out_shape=jax.ShapeDtypeStruct((COMP, ROWS, 1024),...]
    ppermute x8 -> x0, starting transfers between devices: 32.2 us -> none  [the longest x4 16.3 us: extended(): before = lax.ppermute(last, axis, up)]
    sub x36 -> x0, other arithmetic: 29 us -> none  [the longest x32 26.5 us: advance(): two_next = -coef_one * two_now - coef_two * two_prev]
    unnamed x38 -> x0, other arithmetic: 28.2 us -> none
    dynamic_update_slice x32 -> x0, other arithmetic: 25.9 us -> none  [linear_pass(): final, outputs = lax.scan(advance, start, moved, reverse=reverse)]
  transfers between devices with their start and end apart: 9 -> 0, of which waited for: 2 -> 0; matrix products, arithmetic and copies ran while one was open for 4% -> 0% of each run, Pallas kernels for 0% -> 0%
where the time goes in v1:
time: 78.7 us; the launch traced here: 78.2 us
  Pallas kernels  66.5 us (84%)
  local copies, waits for them, and re-layouts  11.7 us (15%)
    pallas_call x1, Pallas kernels, local(): pl.pallas_call(kernel, out_shape=jax.ShapeDtypeStruct((COMP, ROWS, 1024),...  66.5 us
    unnamed x30, local copies, waits for them, and re-layouts  11.7 us

profile of v1, /device:TPU:1, one launch (start us, length us, event | category | flops | bytes accessed | tf_op | source)
XLA Modules:
  0.0 78.2 jit_solution(3834737764222431361)
XLA Ops:
  0.0 0.0 copy-start.13
  0.0 0.0 copy-start.12
  0.0 0.0 copy-start.11
  0.0 0.7 copy-done.13
  0.7 0.0 copy-done.12
  0.7 0.0 copy-done.11
  0.7 0.0 copy-start
  0.7 1.0 %copy-done = f32[5,1,16,1024]{3,2,1,0:T(8,128)S(1)} copy-done((f32[5,1,16,1024]{3,2,1,0:T(8,128)S(1)}, f32[5,1,16,1024]{3,2,1,0:T(8,128)}, u32[]{:S(2)}) %copy-start) | copy-done | bytes 327704
  1.7 0.0 copy-start.1
  1.7 1.0 %copy-done.1 = f32[5,1,16,1024]{3,2,1,0:T(8,128)S(1)} copy-done((f32[5,1,16,1024]{3,2,1,0:T(8,128)S(1)}, f32[5,1,16,1024]{3,2,1,0:T(8,128)}, u32[]{:S(2)}) %copy-start.1) | copy-done | bytes 327704
  2.7 0.0 copy-start.2
  2.7 1.0 %copy-done.2 = f32[5,1,16,1024]{3,2,1,0:T(8,128)S(1)} copy-done((f32[5,1,16,1024]{3,2,1,0:T(8,128)S(1)}, f32[5,1,16,1024]{3,2,1,0:T(8,128)}, u32[]{:S(2)}) %copy-start.2) | copy-done | bytes 327704
  3.7 0.0 copy-start.3
  3.7 1.0 %copy-done.3 = f32[5,1,16,1024]{3,2,1,0:T(8,128)S(1)} copy-done((f32[5,1,16,1024]{3,2,1,0:T(8,128)S(1)}, f32[5,1,16,1024]{3,2,1,0:T(8,128)}, u32[]{:S(2)}) %copy-start.3) | copy-done | bytes 327704
  4.6 0.0 copy-start.4
  4.6 1.0 %copy-done.4 = f32[5,1,16,1024]{3,2,1,0:T(8,128)S(1)} copy-done((f32[5,1,16,1024]{3,2,1,0:T(8,128)S(1)}, f32[5,1,16,1024]{3,2,1,0:T(8,128)}, u32[]{:S(2)}) %copy-start.4) | copy-done | bytes 327704
  5.6 0.0 copy-start.5
  5.6 1.0 %copy-done.5 = f32[5,1,16,1024]{3,2,1,0:T(8,128)S(1)} copy-done((f32[5,1,16,1024]{3,2,1,0:T(8,128)S(1)}, f32[5,1,16,1024]{3,2,1,0:T(8,128)}, u32[]{:S(2)}) %copy-start.5) | copy-done | bytes 327704
  6.6 0.0 copy-start.6
  6.6 0.9 %copy-done.6 = f32[5,5,1,1024]{3,2,1,0:T(1,128)S(1)} copy-done((f32[5,5,1,1024]{3,2,1,0:T(1,128)S(1)}, f32[5,5,1,1024]{3,2,1,0:T(1,128)}, u32[]{:S(2)}) %copy-start.6) | copy-done | bytes 102424
  7.5 0.0 copy-start.7
  7.5 0.9 %copy-done.7 = f32[5,5,1,1024]{3,2,1,0:T(1,128)S(1)} copy-done((f32[5,5,1,1024]{3,2,1,0:T(1,128)S(1)}, f32[5,5,1,1024]{3,2,1,0:T(1,128)}, u32[]{:S(2)}) %copy-start.7) | copy-done | bytes 102424
  8.4 0.0 copy-start.8
  8.4 0.9 %copy-done.8 = s32[8,1,24,128]{3,2,1,0:T(8,128)S(1)} copy-done((s32[8,1,24,128]{3,2,1,0:T(8,128)S(1)}, s32[8,1,24,128]{3,2,1,0:T(8,128)}, u32[]{:S(2)}) %copy-start.8) | copy-done | bytes 98328
  9.3 0.0 copy-start.9
  9.3 0.9 %copy-done.9 = f32[8,1,24,128]{3,2,1,0:T(8,128)S(1)} copy-done((f32[8,1,24,128]{3,2,1,0:T(8,128)S(1)}, f32[8,1,24,128]{3,2,1,0:T(8,128)}, u32[]{:S(2)}) %copy-start.9) | copy-done | bytes 98328
  10.2 0.0 copy-start.10
  10.2 0.8 %copy-done.10 = s32[1,16,1024]{2,1,0:T(8,128)S(1)} copy-done((s32[1,16,1024]{2,1,0:T(8,128)S(1)}, s32[1,16,1024]{2,1,0:T(8,128)}, u32[]{:S(2)}) %copy-start.10) | copy-done | bytes 65560
  11.0 66.5 %adi_window.1 = f32[5,16,1024]{2,1,0:T(8,128)S(1)} custom-call(f32[5,16,1024]{2,1,0:T(8,128)S(1)} %bitcast.20, s32[16,1024]{1,0:T(8,128)S(1)} %bitcast.30, f32[5,5]{1,0:T(8,128)S(1)} %bitcast.31, f32[25,8,128]{2,1,0:T(8,128)S(1)} %bitcast.26, f32[25,8,128]{2,1,0:T(8,128)S(1)} %bitcast.27, f32[5,16,1024]{2,1,0:T(8,128)S(1)} %bitcast.21, ...), custom_call_target="tpu_custom_call" | custom-call | tf_op jit(solution)/shard_map/adi_window/pallas_call | solution.py:709
  77.5 0.7 copy.20
  (1 shorter events, 0.0 us)
Async XLA Ops:
  0.0 0.7 copy-start.13
  0.0 0.7 copy-start.12
  0.0 0.7 copy-start.11
  0.7 1.0 %copy-start = (f32[5,1,16,1024]{3,2,1,0:T(8,128)S(1)}, f32[5,1,16,1024]{3,2,1,0:T(8,128)}, u32[]{:S(2)}) copy-start(f32[5,1,16,1024]{3,2,1,0:T(8,128)} %param.14) | copy-start | bytes 983044
  1.7 1.0 %copy-start.1 = (f32[5,1,16,1024]{3,2,1,0:T(8,128)S(1)}, f32[5,1,16,1024]{3,2,1,0:T(8,128)}, u32[]{:S(2)}) copy-start(f32[5,1,16,1024]{3,2,1,0:T(8,128)} %param.19) | copy-start | bytes 983044
  2.7 1.0 %copy-start.2 = (f32[5,1,16,1024]{3,2,1,0:T(8,128)S(1)}, f32[5,1,16,1024]{3,2,1,0:T(8,128)}, u32[]{:S(2)}) copy-start(f32[5,1,16,1024]{3,2,1,0:T(8,128)} %param.20) | copy-start | bytes 983044
  3.7 1.0 %copy-start.3 = (f32[5,1,16,1024]{3,2,1,0:T(8,128)S(1)}, f32[5,1,16,1024]{3,2,1,0:T(8,128)}, u32[]{:S(2)}) copy-start(f32[5,1,16,1024]{3,2,1,0:T(8,128)} %param.21) | copy-start | bytes 983044
  4.6 1.0 %copy-start.4 = (f32[5,1,16,1024]{3,2,1,0:T(8,128)S(1)}, f32[5,1,16,1024]{3,2,1,0:T(8,128)}, u32[]{:S(2)}) copy-start(f32[5,1,16,1024]{3,2,1,0:T(8,128)} %param.22) | copy-start | bytes 983044
  5.6 1.0 %copy-start.5 = (f32[5,1,16,1024]{3,2,1,0:T(8,128)S(1)}, f32[5,1,16,1024]{3,2,1,0:T(8,128)}, u32[]{:S(2)}) copy-start(f32[5,1,16,1024]{3,2,1,0:T(8,128)} %param.23) | copy-start | bytes 983044
  6.6 0.9 %copy-start.6 = (f32[5,5,1,1024]{3,2,1,0:T(1,128)S(1)}, f32[5,5,1,1024]{3,2,1,0:T(1,128)}, u32[]{:S(2)}) copy-start(f32[5,5,1,1024]{3,2,1,0:T(1,128)} %param.17) | copy-start | bytes 307204
  7.5 0.9 %copy-start.7 = (f32[5,5,1,1024]{3,2,1,0:T(1,128)S(1)}, f32[5,5,1,1024]{3,2,1,0:T(1,128)}, u32[]{:S(2)}) copy-start(f32[5,5,1,1024]{3,2,1,0:T(1,128)} %param.18) | copy-start | bytes 307204
  8.4 0.9 %copy-start.8 = (s32[8,1,24,128]{3,2,1,0:T(8,128)S(1)}, s32[8,1,24,128]{3,2,1,0:T(8,128)}, u32[]{:S(2)}) copy-start(s32[8,1,24,128]{3,2,1,0:T(8,128)} %param.24) | copy-start | bytes 294916
  9.3 0.9 %copy-start.9 = (f32[8,1,24,128]{3,2,1,0:T(8,128)S(1)}, f32[8,1,24,128]{3,2,1,0:T(8,128)}, u32[]{:S(2)}) copy-start(f32[8,1,24,128]{3,2,1,0:T(8,128)} %param.25) | copy-start | bytes 294916
  10.2 0.8 %copy-start.10 = (s32[1,16,1024]{2,1,0:T(8,128)S(1)}, s32[1,16,1024]{2,1,0:T(8,128)}, u32[]{:S(2)}) copy-start(s32[1,16,1024]{2,1,0:T(8,128)} %param.15) | copy-start | bytes 196612

commit v2 on v1

--- a/solution.py
+++ b/solution.py
@@ -10,6 +10,7 @@
 SPANS = 4
 NORMALS = 16
 CAP = 6
+SLOT_ROWS = GRIDS * CAP
 ROWS = 16
 COMP = 5
 LINE = 40
@@ -84,7 +85,6 @@
     one_rows,
     two_rows,
     table,
-    onehots,
     inverse,
     inv_row,
     inv_lane,
@@ -271,6 +271,29 @@
             device_id_type=pl.DeviceIdType.MESH,
         )
 
+    def one_hot_pair(row, pair, total):
+        cells = [cells_v[pl.ds((2 * pair + e) * SLOT_ROWS + row, 1), :] for e in range(2)]
+        parts = []
+        for cell in cells:
+            low = ((cell >> 10) & 1) * 128 + (cell & 127)
+            low = jnp.broadcast_to(low.astype(F32).astype(BF16), (256, 128))
+            rank = iota((256, 128), 0).astype(F32).astype(BF16)
+            parts.append(jnp.where(rank == low, jnp.ones((), BF16), jnp.zeros((), BF16)))
+        hot = jnp.concatenate(parts, axis=1)
+        found = jnp.dot(
+            table[...], jnp.concatenate([hot, hot], axis=0), preferred_element_type=F32
+        )
+        for e in range(2):
+            high = ((cells[e] >> 11) << 3) | ((cells[e] >> 7) & 7)
+            weight = jnp.broadcast_to(
+                weights_v[pl.ds((2 * pair + e) * SLOT_ROWS + row, 1), :], (8, 128)
+            )
+            for v in range(8):
+                mask = jnp.where(iota((8, 128), 0) + v * 8 == high, weight, 0.0)
+                for c in range(COMP):
+                    at = c * 64 + v * 8
+                    total[c] = total[c] + found[at : at + 8, e * 128 : e * 128 + 128] * mask
+
     def interpolate(it):
         for c in range(COMP):
             for m in range(0, 8, 2):
@@ -290,48 +313,30 @@
         for turn, k in enumerate(ORDER):
             receiver = lax.rem(g + k, GRIDS)
 
-            def one_row(b, _, k=k, receiver=receiver):
-                row = receiver * CAP + b
-                total = [zeros8] * COMP
-                for pair in range(4):
-                    cells = [cells_v[2 * pair + e, pl.ds(row, 1), :] for e in range(2)]
-                    if it == 0:
-                        parts = []
-                        for cell in cells:
-                            low = ((cell >> 10) & 1) * 128 + (cell & 127)
-                            low = jnp.broadcast_to(low.astype(F32).astype(BF16), (256, 128))
-                            rank = iota((256, 128), 0).astype(F32).astype(BF16)
-                            parts.append(
-                                jnp.where(rank == low, jnp.ones((), BF16), jnp.zeros((), BF16))
-                            )
-                        hot = jnp.concatenate(parts, axis=1)
-                        onehots[((k - 1) * CAP + b) * 4 + pair] = hot
-                    else:
-                        hot = onehots[((k - 1) * CAP + b) * 4 + pair]
-                    found = jnp.dot(
-                        table[...],
-                        jnp.concatenate([hot, hot], axis=0),
-                        preferred_element_type=F32,
-                    )
-                    for e in range(2):
-                        high = ((cells[e] >> 11) << 3) | ((cells[e] >> 7) & 7)
-                        weight = jnp.broadcast_to(
-                            weights_v[2 * pair + e, pl.ds(row, 1), :], (8, 128)
+            def three_rows(trip, _, k=k, receiver=receiver):
+                first = receiver * CAP + 3 * trip
+                cells = cells_v[pl.ds(first + 2, 8, stride=SLOT_ROWS), :]
+                lanes, blocks = cells & 127, cells >> 7
+                picked = [zeros8] * COMP
+                sums = [[zeros8] * COMP for _ in range(2)]
+                for step in range(8):
+                    one_hot_pair(first + step // 4, step % 4, sums[step // 4])
+                    for block in range(16 * step, 16 * step + 16):
+                        hit = blocks == block
+                        at = (block // 8) * LINE + block % 8
+                        for c in range(COMP):
+                            values = cur[pl.ds(at + c * 8, 8, stride=0), :]
+                            picked[c] = jnp.where(hit, lane_gather(values, lanes), picked[c])
+                weight = weights_v[pl.ds(first + 2, 8, stride=SLOT_ROWS), :]
+                sums.append([p * weight for p in picked])
+                for e in range(3):
+                    for c in range(COMP):
+                        sent[it, k - 1, pl.ds((3 * trip + e) * COMP + c, 1), :] = jnp.sum(
+                            sums[e][c], axis=0, keepdims=True
                         )
-                        for v in range(8):
-                            mask = jnp.where(iota((8, 128), 0) + v * 8 == high, weight, 0.0)
-                            for c in range(COMP):
-                                at = c * 64 + v * 8
-                                total[c] = (
-                                    total[c] + found[at : at + 8, e * 128 : e * 128 + 128] * mask
-                                )
-                for c in range(COMP):
-                    sent[it, k - 1, pl.ds(b * COMP + c, 1), :] = jnp.sum(
-                        total[c], axis=0, keepdims=True
-                    )
                 return 0
 
-            lax.fori_loop(0, CAP, one_row, 0)
+            lax.fori_loop(0, CAP // 3, three_rows, 0)
             if it == 0 and turn == 0:
                 barrier_wait()
             slot_copy(it, k).start()
@@ -410,7 +415,7 @@
     def prepare_mixing():
         loads[10].wait()
         loads[11].wait()
-        f = [[jnp.broadcast_to(flux_v[k, m : m + 1].reshape(1, 1), (8, 128)) for m in range(COMP)] for k in range(COMP)]
+        f = [[jnp.broadcast_to(flux_v[k, :, m : m + 1], (8, 128)) for m in range(COMP)] for k in range(COMP)]
         for c in range(COMP):
             row = [left_v[c * COMP + k] for k in range(COMP)]
             for m in range(COMP):
@@ -714,11 +719,11 @@
         scratch_shapes=[
             vmem(6, COMP, ROWS, 1024),
             vmem(ROWS, 1024, dtype=jnp.int32),
-            vmem(COMP, COMP),
+            vmem(COMP, 1, COMP),
             vmem(25, 8, 128),
             vmem(25, 8, 128),
-            vmem(8, slots, 128, dtype=jnp.int32),
-            vmem(8, slots, 128),
+            vmem(8 * slots, 128, dtype=jnp.int32),
+            vmem(8 * slots, 128),
             vmem(slots, 128, dtype=jnp.int32),
             vmem(slots, 128, dtype=jnp.int32),
             vmem(whole, 128),
@@ -734,7 +739,6 @@
             vmem(whole, 128),
             vmem(whole, 128),
             vmem(320, 512, dtype=BF16),
-            vmem(72, 256, 256, dtype=BF16),
             vmem(256, 128),
             vmem(128, 128, dtype=jnp.int32),
             vmem(128, 128, dtype=jnp.int32),
@@ -770,10 +774,10 @@
             collective_id=0, has_side_effects=True, vmem_limit_bytes=48 << 20
         ),
         name="adi_window",
-    )(
+    )(*(pltpu.with_memory_space_constraint(x, pltpu.HBM) for x in (
         state[:, 0],
         iblank[0],
-        flux[:, :, 0],
+        jnp.swapaxes(flux, 1, 2),
         left_vectors.reshape(25, 8, 128),
         right_vectors.reshape(25, 8, 128),
         low_one[:, 0],
@@ -781,11 +785,11 @@
         up_one[:, 0],
         up_two[:, 0],
         pivot[:, 0],
-        donor_cells[:, 0],
-        donor_weights[:, 0],
+        donor_cells.reshape(8 * slots, 128),
+        donor_weights.reshape(8 * slots, 128),
         fringe_cells[0],
         fringe_live[0],
-    )
+    )))
     return out[:, None]
 
 

time: 78.7 us -> 58.9 us (0.75)
  local copies, waits for them, and re-layouts: 11.7 us -> 0.73 us
  Pallas kernels: 66.5 us -> 58.1 us
    unnamed x30 -> x1, local copies, waits for them, and re-layouts: 11.7 us -> 0.73 us
    pallas_call x1, Pallas kernels: 66.5 us -> 58.1 us  [local(): pl.pallas_call(kernel, out_shape=jax.ShapeDtypeStruct((COMP, ROWS, 1024),...]
where the time goes in v2:
time: 58.9 us; the launch traced here: 58.8 us
  Pallas kernels  58.1 us (99%)
  local copies, waits for them, and re-layouts  0.73 us (1%)
    pallas_call x1, Pallas kernels, local(): pl.pallas_call(kernel, out_shape=jax.ShapeDtypeStruct((COMP, ROWS, 1024),...  58.1 us

profile of v2, /device:TPU:1, one launch (start us, length us, event | category | flops | bytes accessed | tf_op | source)
XLA Modules:
  0.0 58.8 jit_solution(18067716282607234206)
XLA Ops:
  0.0 58.1 %adi_window.1 = f32[5,16,1024]{2,1,0:T(8,128)S(1)} custom-call(f32[5,16,1024]{2,1,0:T(8,128)} %bitcast.18, s32[16,1024]{1,0:T(8,128)} %bitcast.28, f32[5,1,5]{2,1,0:T(1,128)} %bitcast.31, f32[25,8,128]{2,1,0:T(8,128)} %bitcast.24, f32[25,8,128]{2,1,0:T(8,128)} %bitcast.25, f32[5,16,1024]{2,1,0:T(8,128)} %bitcast.19, f32[5,16,1024]{2,1,0:T(8,128)} %bitcast.20, ...), custom_call_target="tpu_custom_call" | custom-call | tf_op jit(solution)/shard_map/adi_window/pallas_call | solution.py:714
  58.1 0.7 %copy.17 = f32[5,1,16,1024]{3,2,1,0:T(8,128)} copy(f32[5,1,16,1024]{3,2,1,0:T(8,128)S(1)} %bitcast.17) | data formatting | bytes 655360

commit v3 on v2

--- a/solution.py
+++ b/solution.py
@@ -13,6 +13,7 @@
 SLOT_ROWS = GRIDS * CAP
 ROWS = 16
 COMP = 5
+JOBS = 10
 LINE = 40
 ORDER = (2, 1, 3)
 F32, BF16 = jnp.float32, jnp.bfloat16
@@ -33,6 +34,15 @@
         slice_sizes=(1, 1),
         mode=lax.GatherScatterMode.PROMISE_IN_BOUNDS,
     )
+
+
+def leader_of(job):
+    return lax.div(8 * job, 5) if not isinstance(job, int) else 8 * job // 5
+
+
+def pack(x, y):
+    upper = iota((8, 128), 0) < 4
+    return jnp.where(upper, x, pltpu.roll(y, 4, 0)), jnp.where(upper, pltpu.roll(x, 4, 0), y)
 
 
 def iota(shape, dim):
@@ -119,8 +129,9 @@
     g = lax.axis_index("grid")
     s = lax.axis_index("span")
     n = lax.axis_index("normal")
-    leader = jnp.logical_and(lax.rem(n, 3) == 0, n < 15)
-    comp_me = lax.div(n, 3)
+    job = lax.div(5 * n + 7, 8)
+    leader = jnp.logical_and(job < JOBS, leader_of(job) == n)
+    visits = [lax.rem(lax.div(5 * n, 8) + off, JOBS) for off in (5, 4, 6, 3, 7, 2, 8, 1, 9, 0)]
 
     pairs = [
         (state, raw.at[0]),
@@ -211,64 +222,40 @@
             device_id_type=pl.DeviceIdType.MESH,
         )
 
-    def mat_copy(c):
+    def to_leader(source, target, ssem, rsem, peer):
         return pltpu.make_async_remote_copy(
-            src_ref=mats.at[c],
-            dst_ref=mats_in.at[n],
-            send_sem=mat_ssem.at[c],
-            recv_sem=mat_rsem.at[n],
-            device_id={"normal": 3 * c},
+            src_ref=source,
+            dst_ref=target,
+            send_sem=ssem,
+            recv_sem=rsem,
+            device_id={"normal": peer},
             device_id_type=pl.DeviceIdType.MESH,
         )
 
-    def b_copy(it, c):
-        return pltpu.make_async_remote_copy(
-            src_ref=bounds.at[it, c],
-            dst_ref=bounds_in.at[it, n],
-            send_sem=b_ssem.at[it, c],
-            recv_sem=b_rsem.at[it, n],
-            device_id={"normal": 3 * c},
-            device_id_type=pl.DeviceIdType.MESH,
+    def mat_copy(j):
+        return to_leader(mats.at[j], mats_in.at[n], mat_ssem.at[j], mat_rsem.at[n], leader_of(j))
+
+    def mat_arrival(k):
+        return to_leader(mats.at[0], mats_in.at[k], mat_ssem.at[0], mat_rsem.at[k], k)
+
+    def b_copy(it, j):
+        return to_leader(
+            bounds.at[it, j], bounds_in.at[it, n], b_ssem.at[it, j], b_rsem.at[it, n], leader_of(j)
         )
 
     def b_arrival(it, k):
-        return pltpu.make_async_remote_copy(
-            src_ref=bounds.at[it, 0],
-            dst_ref=bounds_in.at[it, k],
-            send_sem=b_ssem.at[it, 0],
-            recv_sem=b_rsem.at[it, k],
-            device_id={"normal": k},
-            device_id_type=pl.DeviceIdType.MESH,
+        return to_leader(
+            bounds.at[it, 0], bounds_in.at[it, k], b_ssem.at[it, 0], b_rsem.at[it, k], k
         )
 
-    def mat_arrival(k):
-        return pltpu.make_async_remote_copy(
-            src_ref=mats.at[0],
-            dst_ref=mats_in.at[k],
-            send_sem=mat_ssem.at[0],
-            recv_sem=mat_rsem.at[k],
-            device_id={"normal": k},
-            device_id_type=pl.DeviceIdType.MESH,
+    def e_copy(it, k):
+        return to_leader(
+            enter_out.at[it, k], enter.at[it, job], e_ssem.at[it, k], e_rsem.at[it, job], k
         )
 
-    def e_copy(it, k):
-        return pltpu.make_async_remote_copy(
-            src_ref=enter_out.at[it, k],
-            dst_ref=enter.at[it, comp_me],
-            send_sem=e_ssem.at[it, k],
-            recv_sem=e_rsem.at[it, comp_me],
-            device_id={"normal": k},
-            device_id_type=pl.DeviceIdType.MESH,
-        )
-
-    def e_arrival(it, c):
-        return pltpu.make_async_remote_copy(
-            src_ref=enter_out.at[it, 0],
-            dst_ref=enter.at[it, c],
-            send_sem=e_ssem.at[it, 0],
-            recv_sem=e_rsem.at[it, c],
-            device_id={"normal": 3 * c},
-            device_id_type=pl.DeviceIdType.MESH,
+    def e_arrival(it, j):
+        return to_leader(
+            enter_out.at[it, 0], enter.at[it, j], e_ssem.at[it, 0], e_rsem.at[it, j], leader_of(j)
         )
 
     def one_hot_pair(row, pair, total):
@@ -338,31 +325,40 @@
 
             lax.fori_loop(0, CAP // 3, three_rows, 0)
             if it == 0 and turn == 0:
+                load_coefficients()
                 barrier_wait()
             slot_copy(it, k).start()
+            if it == 0 and turn == 0:
+                send_matrices()
 
     def invert_fringe():
-        inverse[...] = jnp.zeros((256, 128), F32)
+        total = jnp.zeros((256, 128), F32)
+        lane = iota((128, 128), 1).astype(F32)
+        place_of = iota((128, 128), 0)
         for k in ORDER:
             source = lax.rem(g + GRIDS - k, GRIDS)
-
-            def one(b, _, k=k, source=source):
+            named, columns = [], []
+            for b in range(CAP):
                 row = source * CAP + b
                 cell = fringe_v[pl.ds(row, 1), :]
                 live = live_v[pl.ds(row, 1), :]
                 high = jnp.where(live == 1, cell >> 7, -1)
                 low = cell & 127
-                number = (((k - 1) * CAP + b) + 1).astype(F32)
-                at = jnp.where(iota((128, 128), 0) == high, 1.0, 0.0)
-                lane = iota((128, 128), 1).astype(F32)
-                a = jnp.concatenate([at * number, at * lane], axis=0).astype(BF16)
-                col = jnp.where(iota((128, 128), 0) == low, 1.0, 0.0).astype(BF16)
-                inverse[...] += lax.dot_general(
-                    a, col, (((1,), (1,)), ((), ())), preferred_element_type=F32
+                hit = place_of == high
+                number = float((k - 1) * CAP + b + 1)
+                named.append(
+                    jnp.concatenate(
+                        [jnp.where(hit, number, 0.0), jnp.where(hit, lane, 0.0)], axis=0
+                    ).astype(BF16)
                 )
-                return 0
-
-            lax.fori_loop(0, CAP, one, 0)
+                columns.append(jnp.where(place_of == low, 1.0, 0.0).astype(BF16))
+            total = total + lax.dot_general(
+                jnp.concatenate(named, axis=1),
+                jnp.concatenate(columns, axis=1),
+                (((1,), (1,)), ((), ())),
+                preferred_element_type=F32,
+            )
+        inverse[...] = total
         inv_row[...] = inverse[0:128, :].astype(jnp.int32) - 1
         inv_lane[...] = inverse[128:256, :].astype(jnp.int32)
 
@@ -390,24 +386,31 @@
             q1, q2 = pv * line(two_rows, i) - c1 * q1 - c2 * q2, q1
         found += [a1, b1, a2, b2, p1, q1, p2, q2]
         for c in range(COMP):
-            for j, whole in enumerate(found):
-                mats[c, j] = whole[c * 8 : c * 8 + 8, :]
-
-    def prepare():
+            part = [whole[c * 8 : c * 8 + 8, :] for whole in found]
+            for j in range(0, 12, 4):
+                for half, packed in enumerate(pack(part[j], part[j + 3])):
+                    mats[2 * c + half, j // 2] = packed
+                for half, packed in enumerate(pack(part[j + 1], part[j + 2])):
+                    mats[2 * c + half, j // 2 + 1] = packed
+
+    def load_coefficients():
         for k, lines in ((3, low1), (4, low2), (5, up1), (6, up2), (7, piv)):
             loads[k].wait()
             to_lines(raw.at[k - 2], lines)
         block_matrices()
-        for c in range(COMP):
-
-            @pl.when(n != 3 * c)
-            def _(c=c):
-                mat_copy(c).start()
+
+    def send_matrices():
+        for j in visits:
+
+            @pl.when(leader_of(j) != n)
+            def _(j=j):
+                mat_copy(j).start()
 
         @pl.when(leader)
         def _():
-            mats_in[n] = mats[comp_me]
-
+            mats_in[n] = mats[job]
+
+    def prepare():
         loads[8].wait()
         loads[9].wait()
         invert_fringe()
@@ -545,62 +548,58 @@
             return 0
 
         lax.fori_loop(0, NORMALS, arrive, 0)
-        e1 = e2 = zeros8
+        def apply(k, at, x):
+            return mats_in[k, at] * x + mats_in[k, at + 1] * pltpu.roll(x, 4, 0)
+
+        x = zeros8
         pushed = []
         for k in range(NORMALS):
-            enter_out[it, k, 0] = e1
-            enter_out[it, k, 1] = e2
-            pushed.append(
-                (
-                    mats_in[k, 8] * e1 + mats_in[k, 9] * e2 + bounds_in[it, k, 2],
-                    mats_in[k, 10] * e1 + mats_in[k, 11] * e2 + bounds_in[it, k, 3],
-                )
-            )
-            e1, e2 = (
-                mats_in[k, 0] * e1 + mats_in[k, 1] * e2 + bounds_in[it, k, 0],
-                mats_in[k, 2] * e1 + mats_in[k, 3] * e2 + bounds_in[it, k, 1],
-            )
-        f1 = f2 = zeros8
+            enter_out[it, k, 0] = x
+            pushed.append(apply(k, 4, x) + bounds_in[it, k, 1])
+            x = apply(k, 0, x) + bounds_in[it, k, 0]
+        x = zeros8
         for k in reversed(range(NORMALS)):
-            enter_out[it, k, 2] = f1
-            enter_out[it, k, 3] = f2
-            f1, f2 = (
-                mats_in[k, 4] * f1 + mats_in[k, 5] * f2 + pushed[k][0],
-                mats_in[k, 6] * f1 + mats_in[k, 7] * f2 + pushed[k][1],
-            )
+            enter_out[it, k, 1] = x
+            x = apply(k, 2, x) + pushed[k]
         for far in range(8, 0, -1):
             for off in {far, NORMALS - far}:
                 e_copy(it, lax.rem(n + off, NORMALS)).start()
-        enter[it, comp_me] = enter_out[it, n]
+        enter[it, job] = enter_out[it, n]
 
     def lines_step(it):
         zero = jnp.zeros((LINE, 128), F32)
         found = sweep(zero, zero, zero, zero)
         for c in range(COMP):
-            for j, whole in enumerate(found):
-                bounds[it, c, j] = whole[c * 8 : c * 8 + 8, :]
-        for c in range(COMP):
-
-            @pl.when(n != 3 * c)
-            def _(c=c):
-                b_copy(it, c).start()
+            part = [whole[c * 8 : c * 8 + 8, :] for whole in found]
+            for way in range(2):
+                for half, packed in enumerate(pack(part[2 * way], part[2 * way + 1])):
+                    bounds[it, 2 * c + half, way] = packed
+        for j in visits:
+
+            @pl.when(leader_of(j) != n)
+            def _(j=j):
+                b_copy(it, j).start()
 
         @pl.when(leader)
         def _():
-            bounds_in[it, n] = bounds[it, comp_me]
+            bounds_in[it, n] = bounds[it, job]
             lead(it)
 
         if it == 0:
             finish_loads()
+        for j in range(JOBS):
+
+            @pl.when(n != leader_of(j))
+            def _(j=j):
+                e_arrival(it, j).wait_recv()
+
+        entering = [[], [], [], []]
         for c in range(COMP):
-
-            @pl.when(n != 3 * c)
-            def _(c=c):
-                e_arrival(it, c).wait_recv()
-
-        entering = [
-            jnp.concatenate([enter[it, c, j] for c in range(COMP)], axis=0) for j in range(4)
-        ]
+            for way in range(2):
+                x, y = pack(enter[it, 2 * c, way], enter[it, 2 * c + 1, way])
+                entering[2 * way].append(x)
+                entering[2 * way + 1].append(y)
+        entering = [jnp.concatenate(parts, axis=0) for parts in entering]
         sweep(*entering)
 
     def finish_loads():
@@ -674,13 +673,13 @@
         def _(it=it):
             y_copy(it, 1).wait_send()
 
-        for c in range(COMP):
-
-            @pl.when(n != 3 * c)
-            def _(c=c, it=it):
+        for j in range(JOBS):
+
+            @pl.when(n != leader_of(j))
+            def _(j=j, it=it):
                 if it == 0:
-                    mat_copy(c).wait_send()
-                b_copy(it, c).wait_send()
+                    mat_copy(j).wait_send()
+                b_copy(it, j).wait_send()
 
         @pl.when(leader)
         def _(it=it):
@@ -750,12 +749,12 @@
             vmem(80, 128),
             vmem(ITERS, 2 * LINE, 128),
             vmem(ITERS, 2 * LINE, 128),
-            vmem(COMP, 12, 8, 128),
-            vmem(NORMALS, 12, 8, 128),
-            vmem(ITERS, COMP, 4, 8, 128),
-            vmem(ITERS, NORMALS, 4, 8, 128),
-            vmem(ITERS, NORMALS, 4, 8, 128),
-            vmem(ITERS, COMP, 4, 8, 128),
+            vmem(JOBS, 6, 8, 128),
+            vmem(NORMALS, 6, 8, 128),
+            vmem(ITERS, JOBS, 2, 8, 128),
+            vmem(ITERS, NORMALS, 2, 8, 128),
+            vmem(ITERS, NORMALS, 2, 8, 128),
+            vmem(ITERS, JOBS, 2, 8, 128),
             dma((14,)),
             dma((ITERS, 3)),
             dma((ITERS, 3)),
@@ -763,12 +762,12 @@
             dma((ITERS, 2)),
             dma((ITERS, 2)),
             dma((ITERS, 2)),
-            dma((COMP,)),
+            dma((JOBS,)),
             dma((NORMALS,)),
-            dma((ITERS, COMP)),
+            dma((ITERS, JOBS)),
             dma((ITERS, NORMALS)),
             dma((ITERS, NORMALS)),
-            dma((ITERS, COMP)),
+            dma((ITERS, JOBS)),
         ],
         compiler_params=pltpu.CompilerParams(
             collective_id=0, has_side_effects=True, vmem_limit_bytes=48 << 20

time: 58.9 us -> 55.7 us (0.946)
  Pallas kernels: 58.1 us -> 54.8 us
    pallas_call x1, Pallas kernels: 58.1 us -> 54.8 us  [local(): pl.pallas_call(kernel, out_shape=jax.ShapeDtypeStruct((COMP, ROWS, 1024),...]
where the time goes in v3:
time: 55.7 us; the launch traced here: 55.6 us
  Pallas kernels  54.8 us (98%)
  local copies, waits for them, and re-layouts  0.73 us (1%)
    pallas_call x1, Pallas kernels, local(): pl.pallas_call(kernel, out_shape=jax.ShapeDtypeStruct((COMP, ROWS, 1024),...  54.8 us

profile of v3, /device:TPU:1, one launch (start us, length us, event | category | flops | bytes accessed | tf_op | source)
XLA Modules:
  0.0 55.6 jit_solution(1585325475684429770)
XLA Ops:
  0.0 54.8 %adi_window.1 = f32[5,16,1024]{2,1,0:T(8,128)S(1)} custom-call(f32[5,16,1024]{2,1,0:T(8,128)} %bitcast.18, s32[16,1024]{1,0:T(8,128)} %bitcast.28, f32[5,1,5]{2,1,0:T(1,128)} %bitcast.31, f32[25,8,128]{2,1,0:T(8,128)} %bitcast.24, f32[25,8,128]{2,1,0:T(8,128)} %bitcast.25, f32[5,16,1024]{2,1,0:T(8,128)} %bitcast.19, f32[5,16,1024]{2,1,0:T(8,128)} %bitcast.20, ...), custom_call_target="tpu_custom_call" | custom-call | tf_op jit(solution)/shard_map/adi_window/pallas_call | solution.py:713
  54.8 0.7 %copy.17 = f32[5,1,16,1024]{3,2,1,0:T(8,128)} copy(f32[5,1,16,1024]{3,2,1,0:T(8,128)S(1)} %bitcast.17) | data formatting | bytes 655360

commit v4 on v3

--- a/solution.py
+++ b/solution.py
@@ -192,12 +192,12 @@
     loads[1].wait()
     loads[2].wait()
 
-    def slot_copy(it, k):
+    def slot_copy(it, k, half):
         return pltpu.make_async_remote_copy(
-            src_ref=sent.at[it, k - 1],
-            dst_ref=received.at[it, k - 1],
-            send_sem=slot_ssem.at[it, k - 1],
-            recv_sem=slot_rsem.at[it, k - 1],
+            src_ref=sent.at[it, k - 1, half],
+            dst_ref=received.at[it, k - 1, half],
+            send_sem=slot_ssem.at[it, k - 1, half],
+            recv_sem=slot_rsem.at[it, k - 1, half],
             device_id={"grid": lax.rem(g + k, GRIDS)},
             device_id_type=pl.DeviceIdType.MESH,
         )
@@ -300,7 +300,7 @@
         for turn, k in enumerate(ORDER):
             receiver = lax.rem(g + k, GRIDS)
 
-            def three_rows(trip, _, k=k, receiver=receiver):
+            def three_rows(trip, _, k=k, receiver=receiver, turn=turn):
                 first = receiver * CAP + 3 * trip
                 cells = cells_v[pl.ds(first + 2, 8, stride=SLOT_ROWS), :]
                 lanes, blocks = cells & 127, cells >> 7
@@ -318,17 +318,19 @@
                 sums.append([p * weight for p in picked])
                 for e in range(3):
                     for c in range(COMP):
-                        sent[it, k - 1, pl.ds((3 * trip + e) * COMP + c, 1), :] = jnp.sum(
+                        sent[it, k - 1, trip, e * COMP + c : e * COMP + c + 1, :] = jnp.sum(
                             sums[e][c], axis=0, keepdims=True
                         )
+                if it > 0 or turn > 0:
+                    slot_copy(it, k, trip).start()
                 return 0
 
             lax.fori_loop(0, CAP // 3, three_rows, 0)
             if it == 0 and turn == 0:
                 load_coefficients()
                 barrier_wait()
-            slot_copy(it, k).start()
-            if it == 0 and turn == 0:
+                for half in range(2):
+                    slot_copy(it, k, half).start()
                 send_matrices()
 
     def invert_fringe():
@@ -428,28 +430,29 @@
                 mix_c[c * COMP + m] = total * -0.2
                 mix_d[c * COMP + m] = row[m] * -0.024
 
-    def place_rows(it, k, i_list):
+    def place_rows(it, k, half, i_list):
         for i in i_list:
             lanes = inv_lane[i * 8 : i * 8 + 8, :]
             rows = inv_row[i * 8 : i * 8 + 8, :]
             values = [cur[i * LINE + c * 8 : i * LINE + c * 8 + 8, :] for c in range(COMP)]
-            for b in range(CAP):
-                hit = rows == (k - 1) * CAP + b
+            for b in range(CAP // 2):
+                hit = rows == (k - 1) * CAP + half * (CAP // 2) + b
                 for c in range(COMP):
-                    slots = received[it, k - 1, pl.ds(b * COMP + c, 8, stride=0), :]
+                    slots = received[it, k - 1, half, pl.ds(b * COMP + c, 8, stride=0), :]
                     values[c] = jnp.where(hit, lane_gather(slots, lanes), values[c])
             for c in range(COMP):
                 cur[i * LINE + c * 8 : i * LINE + c * 8 + 8, :] = values[c]
 
     def place(it):
         for turn, k in enumerate(ORDER):
-            slot_copy(it, k).wait_recv()
-            if turn == GRIDS - 2:
-                place_rows(it, k, (0, 1, 14, 15))
-                start_z(it)
-                place_rows(it, k, range(2, 14))
-            else:
-                place_rows(it, k, range(ROWS))
+            for half in range(2):
+                slot_copy(it, k, half).wait_recv()
+                if turn == GRIDS - 2 and half == 1:
+                    place_rows(it, k, half, (0, 1, 14, 15))
+                    start_z(it)
+                    place_rows(it, k, half, range(2, 14))
+                else:
+                    place_rows(it, k, half, range(ROWS))
 
     def start_z(it):
         @pl.when(n < NORMALS - 1)
@@ -663,7 +666,8 @@
 
     for it in range(ITERS):
         for k in ORDER:
-            slot_copy(it, k).wait_send()
+            for half in range(2):
+                slot_copy(it, k, half).wait_send()
 
         @pl.when(s < SPANS - 1)
         def _(it=it):
@@ -741,8 +745,8 @@
             vmem(256, 128),
             vmem(128, 128, dtype=jnp.int32),
             vmem(128, 128, dtype=jnp.int32),
-            vmem(ITERS, 3, CAP * COMP, 128),
-            vmem(ITERS, 3, CAP * COMP, 128),
+            vmem(ITERS, 3, 2, CAP // 2 * COMP, 128),
+            vmem(ITERS, 3, 2, CAP // 2 * COMP, 128),
             vmem(ITERS, 2, 8, 128),
             vmem(ITERS, 2, 8, 128),
             vmem(80, 128),
@@ -756,8 +760,8 @@
             vmem(ITERS, NORMALS, 2, 8, 128),
             vmem(ITERS, JOBS, 2, 8, 128),
             dma((14,)),
-            dma((ITERS, 3)),
-            dma((ITERS, 3)),
+            dma((ITERS, 3, 2)),
+            dma((ITERS, 3, 2)),
             dma((ITERS, 2)),
             dma((ITERS, 2)),
             dma((ITERS, 2)),

time: 55.7 us -> 55.2 us (level)
  no operation moved by 1% of the time
where the time goes in v4:
time: 55.2 us; the launch traced here: 55.1 us
  Pallas kernels  54.3 us (98%)
  local copies, waits for them, and re-layouts  0.73 us (1%)
    pallas_call x1, Pallas kernels, local(): pl.pallas_call(kernel, out_shape=jax.ShapeDtypeStruct((COMP, ROWS, 1024),...  54.3 us

profile of v4, /device:TPU:1, one launch (start us, length us, event | category | flops | bytes accessed | tf_op | source)
XLA Modules:
  0.0 55.1 jit_solution(16372635237202830034)
XLA Ops:
  0.0 54.3 %adi_window.1 = f32[5,16,1024]{2,1,0:T(8,128)S(1)} custom-call(f32[5,16,1024]{2,1,0:T(8,128)} %bitcast.18, s32[16,1024]{1,0:T(8,128)} %bitcast.28, f32[5,1,5]{2,1,0:T(1,128)} %bitcast.31, f32[25,8,128]{2,1,0:T(8,128)} %bitcast.24, f32[25,8,128]{2,1,0:T(8,128)} %bitcast.25, f32[5,16,1024]{2,1,0:T(8,128)} %bitcast.19, f32[5,16,1024]{2,1,0:T(8,128)} %bitcast.20, ...), custom_call_target="tpu_custom_call" | custom-call | tf_op jit(solution)/shard_map/adi_window/pallas_call | solution.py:717
  54.3 0.7 %copy.17 = f32[5,1,16,1024]{3,2,1,0:T(8,128)} copy(f32[5,1,16,1024]{3,2,1,0:T(8,128)S(1)} %bitcast.17) | data formatting | bytes 655360
